TPU v7x, 256 devices: a whole 4x4x8 slice. The times are simulated.
256 devices in a mesh: expert: 32 (over x, z), dp: 8 (over y, core).
Axes of the slice: x: 4, y: 4, z: 8, core: 2. Of those that a mesh axis runs over, the one named last changes fastest.
Arguments:
- tokens: bfloat16 [32768, 2560], P(('expert', 'dp')), may hold values from -6 to 6
- routing: int32 [32768, 6], P(('expert', 'dp')), may hold values from 0 to 31, all different within a row; in each aligned block of 128 rows (0 to 127, 128 to 255, ...) at most 36 rows name the same one
- grad_up: bfloat16 [32, 9216, 768], P('expert', 'dp'), may hold values from -6 to 6
- up_shard: bfloat16 [32, 2560, 768], P('expert', 'dp'), may hold values from -0.125 to 0.125
- error_feedback: bfloat16 [32, 20480, 768], P('expert', 'dp'), may hold values from -60 to 60
- moment_one: bfloat16 [32, 2560, 768], P('expert', 'dp'), may hold values from -3 to 3
- moment_two: bfloat16 [32, 2560, 768], P('expert', 'dp'), may hold values from 0.049804688 to 0.796875
- loss_scale: float32 [], replicated, may hold values from 8 to 32
Outputs:
- grad_tokens: bfloat16 [32768, 2560], P(('expert', 'dp'))
- new_weights: bfloat16 [32, 2560, 768], P('expert')
- new_moment_one: bfloat16 [32, 2560, 768], P('expert', 'dp')
- new_moment_two: bfloat16 [32, 2560, 768], P('expert', 'dp')
Inputs may be any that keep to these rules, and one draw needn't show every extreme that they name: `routing`: each row names 6 different experts; among the 128 rows of one device no expert is named more than 36 times, a bound that some block reaches.
All inputs are finite; a program needn't handle non-finite values.
Results may differ from a plain program's by a relative error of at most 0.0049.
Values may be sent and summed in bfloat16 or wider, within the bound.
No kernel may reach another device: no remote copies, remote signals or barrier semaphores. Data moves between devices by JAX's collectives and lax.ppermute only.
A program may use at most 128 MiB of HBM per device.

v0:
```python
import jax
import jax.numpy as jnp
from jax import lax
from jax.sharding import PartitionSpec as P

D = 2560
FF = 768
TOP = 6
QB = 128
STEP = 20
TOK_DEV = 128


learn_rate = 0.001
beta_one = 0.9
beta_two = 0.999
decay_rate = 0.1
adam_eps = 1e-08
quant_top = 127.0
amax_eps = 1e-06


def place_pairs(routes_block, expert_total):
    chosen = routes_block.reshape(-1)
    onehot = (chosen[:, None] == jnp.arange(expert_total, dtype=jnp.int32)[None, :]).astype(
        jnp.int32
    )
    before = jnp.cumsum(onehot, axis=0) - onehot
    within = jnp.sum(before * onehot, axis=1)
    counts = jnp.sum(onehot, axis=0)
    return (chosen, within, counts)


def dequantized(values):
    row_total, columns = values.shape
    blocks = values.reshape(row_total, columns // QB, QB)
    block_scale = ((jnp.max(jnp.abs(blocks), axis=2) + amax_eps) / quant_top).astype(jnp.bfloat16)
    levels = (blocks / block_scale.astype(jnp.float32)[:, :, None]).astype(jnp.bfloat16)
    return (levels, block_scale)


def adam_update(weights, first_moment, second_moment, gradient):
    first_new = beta_one * first_moment.astype(jnp.float32) + (1.0 - beta_one) * gradient
    second_new = (
        beta_two * second_moment.astype(jnp.float32) + (1.0 - beta_two) * gradient * gradient
    )
    first_hat = first_new / (1.0 - beta_one**STEP)
    second_hat = second_new / (1.0 - beta_two**STEP)
    master = weights.astype(jnp.float32)
    updated = master - learn_rate * (
        first_hat / (jnp.sqrt(second_hat) + adam_eps) + decay_rate * master
    )
    return (
        updated.astype(jnp.bfloat16),
        first_new.astype(jnp.bfloat16),
        second_new.astype(jnp.bfloat16),
    )


def on_device(
    tokens, routing, grad_up, up_shard, error_feedback, moment_one, moment_two, loss_scale
):
    experts = lax.axis_size("expert")
    copies = lax.axis_size("dp")
    slot_count = grad_up.shape[1]
    capacity = slot_count // experts
    chosen, within, counts = place_pairs(routing, experts)
    target = chosen * capacity + within
    token_ids = jnp.arange(TOK_DEV * TOP, dtype=jnp.int32) // TOP
    slot_token = jnp.zeros((slot_count,), jnp.int32).at[target].set(token_ids)
    outgoing = tokens[slot_token].reshape(experts, capacity, D)
    count_values = counts.astype(jnp.bfloat16).reshape(experts, 1)
    arrived, arrived_counts = (
        lax.all_to_all(outgoing, "expert", split_axis=0, concat_axis=0, tiled=True),
        lax.all_to_all(count_values, "expert", split_axis=0, concat_axis=0, tiled=True),
    )
    count_ints = arrived_counts.astype(jnp.int32)
    live_slot = (jnp.arange(capacity, dtype=jnp.int32)[None, :] < count_ints).reshape(-1)
    up_rows = grad_up[0]
    masked = jnp.where(live_slot[:, None], up_rows, jnp.zeros_like(up_rows))
    arrived_rows = arrived.reshape(slot_count, D)
    partial_sum = lax.dot_general(
        arrived_rows, masked, (((0,), (0,)), ((), ())), preferred_element_type=jnp.float32
    )
    returned = lax.dot_general(
        masked,
        lax.all_gather(up_shard[0], "dp", axis=0, tiled=True),
        (((1,), (1,)), ((), ())),
        preferred_element_type=jnp.float32,
    ).astype(jnp.bfloat16)
    with_error = partial_sum + error_feedback[0].astype(jnp.float32)
    levels, block_scale = dequantized(with_error)
    shard_rows = D // copies
    got_levels, got_scale = (
        lax.all_to_all(
            levels.reshape(copies, shard_rows, FF), "dp", split_axis=0, concat_axis=0, tiled=True
        ),
        lax.all_to_all(
            block_scale.reshape(copies, shard_rows, FF // QB),
            "dp",
            split_axis=0,
            concat_axis=0,
            tiled=True,
        ),
    )
    summed_grad = jnp.sum(
        got_levels.astype(jnp.float32).reshape(copies, shard_rows, FF // QB, QB)
        * got_scale.astype(jnp.float32)[:, :, :, None],
        axis=0,
    ).reshape(shard_rows, FF)
    gradient = summed_grad / loss_scale
    new_w, new_m, new_v = adam_update(up_shard[0], moment_one[0], moment_two[0], gradient)
    full_weights = lax.all_gather(new_w, "dp", axis=0, tiled=True)
    came_back = lax.all_to_all(
        returned.reshape(experts, capacity, D), "expert", split_axis=0, concat_axis=0, tiled=True
    )
    picked = came_back.reshape(slot_count, D)[target].reshape(TOK_DEV, TOP, D)
    grad_tokens = jnp.sum(picked.astype(jnp.float32), axis=1).astype(jnp.bfloat16)
    return (grad_tokens, full_weights[None], new_m[None], new_v[None])


def solution(mesh):
    in_specs = (
        P(("expert", "dp"), None),
        P(("expert", "dp"), None),
        P("expert", "dp", None),
        P("expert", "dp", None),
        P("expert", "dp", None),
        P("expert", "dp", None),
        P("expert", "dp", None),
        P(),
    )
    out_specs = (
        P(("expert", "dp"), None),
        P("expert", None, None),
        P("expert", "dp", None),
        P("expert", "dp", None),
    )
    return jax.shard_map(
        on_device, mesh=mesh, in_specs=in_specs, out_specs=out_specs, check_vma=False
    )
```

profile of v0, /device:TPU:1, one launch (start us, length us, event | category | flops | bytes accessed | tf_op | source)
XLA Modules:
  0.0 518.6 jit_solution(15999721090822679827)
XLA Ops:
  7.2 0.0 copy-start
  7.2 0.9 copy.78
  8.0 0.1 eq.29
  8.2 0.1 eq.25
  8.3 1.7 reduce-window.6
  10.1 0.3 slice_reduce_fusion
  10.4 0.1 fusion.21
  10.5 0.7 copy.79
  11.2 11.9 %all-to-all-start = ((bf16[32,1,1]{2,1,0:T(2,128)(2,1)}), bf16[32,1,1]{2,1,0:T(2,128)(2,1)S(1)}, u32[]{:S(2)}, u32[]{:S(2)}) async-start(bf16[32,1,1]{2,1,0:T(2,128)(2,1)} %copy.79), calls=%async_computation | async-start | bytes 32768 | tf_op jit(solution)/shard_map/all_to_all | solution.py:75
  23.1 0.7 broadcast_multiply_fusion
  23.8 0.1 copy.80
  23.9 0.1 mul.94
  24.1 3.4 scatter_custom_fusion
  27.5 6.4 %gather_fusion.1 = bf16[1152,2560]{1,0:T(8,128)(2,1)} fusion(bf16[128,2560]{1,0:T(8,128)(2,1)S(1)} %copy-done, s32[2048]{0:T(1024)S(1)} %pad_clamp_fusion), kind=kCustom, calls=%fused_computation.1 | custom fusion | bytes 11801088 | tf_op jit(solution)/shard_map/gather | solution.py:71
  33.9 8.0 %reshape.174 = bf16[32,36,2560]{2,1,0:T(8,128)(2,1)} reshape(bf16[1152,2560]{1,0:T(8,128)(2,1)} %gather_fusion.1) | data formatting | bytes 11796480 | tf_op jit(solution)/shard_map/reshape | solution.py:71
  41.9 0.0 all-to-all-done
  41.9 9.3 %all-to-all-start.2 = ((bf16[32,36,2560]{2,1,0:T(8,128)(2,1)}), bf16[32,36,2560]{2,1,0:T(8,128)(2,1)}, u32[]{:S(2)}, u32[]{:S(2)}) async-start(bf16[32,36,2560]{2,1,0:T(8,128)(2,1)} %reshape.174), calls=%async_computation.2 | async-start | bytes 13107200 | tf_op jit(solution)/shard_map/all_to_all | solution.py:74
  51.2 0.0 all-gather.6.cloned.1.call-start
  51.3 0.7 all-gather.6.cloned.1.call-update
  52.0 0.7 convert_reduce_fusion.1
  52.6 0.1 iota_compare_fusion.2
  52.7 0.1 lt.37
  52.8 0.0 copy-start.5
  52.9 142.9 %all-to-all-done.2 = bf16[32,36,2560]{2,1,0:T(8,128)(2,1)} async-done(((bf16[32,36,2560]{2,1,0:T(8,128)(2,1)}), bf16[32,36,2560]{2,1,0:T(8,128)(2,1)}, u32[]{:S(2)}, u32[]{:S(2)}) %all-to-all-start.2) | async-done | bytes 5898272 | tf_op jit(solution)/shard_map/all_to_all | solution.py:74
  195.7 8.1 %reshape.175 = bf16[1152,2560]{1,0:T(8,128)(2,1)} reshape(bf16[32,36,2560]{2,1,0:T(8,128)(2,1)} %all-to-all-done.2) | data formatting | bytes 11796480 | tf_op jit(solution)/shard_map/reshape | solution.py:81
  203.8 12.2 %fusion.31 = (f32[2560,768]{1,0:T(8,128)}, f32[2560,768]{1,0:T(8,128)}) fusion(bf16[1,2560,768]{2,1,0:T(8,128)(2,1)} %param.12, bf16[1152,2560]{1,0:T(8,128)(2,1)} %reshape.175, bf16[1,1152,768]{2,1,0:T(8,128)(2,1)S(1)} %copy-done.5, pred[1152]{0:T(1024)(128)(4,1)S(1)} %lt.37), kind=kOutput, calls=%fused_computation.68 | convolution fusion | flops 4536631296 | bytes 27329664 | tf_op jit(solution)/shard_map/dot_general | solution.py:82
  216.0 9.1 %copy.85 = f32[2560,768]{0,1:T(8,128)} copy(f32[2560,768]{1,0:T(8,128)} %get-tuple-element.24) | data formatting | bytes 15728640 | tf_op jit(solution)/shard_map/abs | solution.py:37
  225.1 3.8 reduce_max.9
  229.0 0.1 convert_element_type.110
  229.1 4.0 div.61
  233.1 10.0 %div.62 = f32[8,320,768]{1,0,2:T(8,128)} reshape(f32[2560,6,128]{0,2,1:T(8,128)} %div.61) | data formatting | bytes 15728640 | tf_op jit(solution)/shard_map/div | solution.py:38
  243.1 9.2 %copy.86 = f32[8,320,768]{2,1,0:T(8,128)} copy(f32[8,320,768]{1,0,2:T(8,128)} %div.62) | data formatting | bytes 15728640 | tf_op jit(solution)/shard_map/div | solution.py:38
  252.3 0.6 copy.87
  252.9 5.9 %all-to-all-start.4 = ((bf16[8,320,6]{1,2,0:T(8,128)(2,1)}), bf16[8,320,6]{1,2,0:T(8,128)(2,1)S(1)}, u32[]{:S(2)}, u32[]{:S(2)}) async-start(bf16[8,320,6]{1,2,0:T(8,128)(2,1)} %copy.87), calls=%async_computation.4 | async-start | bytes 98304 | tf_op jit(solution)/shard_map/all_to_all | solution.py:98
  258.8 8.6 %divide_convert_fusion = bf16[8,320,768]{2,1,0:T(8,128)(2,1)} fusion(f32[8,320,768]{2,1,0:T(8,128)} %bitcast.57, f32[8,320,768]{2,1,0:T(8,128)} %copy.86), kind=kLoop, calls=%fused_computation.6 | loop fusion | flops 3932160 | bytes 19660800 | tf_op jit(solution)/shard_map/convert_element_type | solution.py:38
  267.4 0.0 all-to-all-done.4
  267.4 4.8 all-to-all-start.3
  272.2 9.0 %convolution_convert_fusion = bf16[1152,2560]{1,0:T(8,128)(2,1)} fusion(bf16[1,2560,768]{2,1,0:T(8,128)(2,1)} %all-gather.6.cloned.1.call-done, bf16[1,1152,768]{2,1,0:T(8,128)(2,1)S(1)} %copy-done.5, pred[1152]{0:T(1024)(128)(4,1)S(1)} %lt.37), kind=kOutput, calls=%fused_computation.3 | convolution fusion | flops 4533682176 | bytes 11601024 | tf_op jit(solution)/shard_map/dot_general | solution.py:85
  281.2 8.1 %reshape.170 = bf16[32,36,2560]{2,1,0:T(8,128)(2,1)} reshape(bf16[1152,2560]{1,0:T(8,128)(2,1)} %convolution_convert_fusion) | data formatting | bytes 11796480 | tf_op jit(solution)/shard_map/reshape | solution.py:115
  289.3 28.8 %all-to-all-done.3 = bf16[8,320,768]{2,1,0:T(8,128)(2,1)} async-done(((bf16[8,320,768]{2,1,0:T(8,128)(2,1)}), bf16[8,320,768]{2,1,0:T(8,128)(2,1)}, u32[]{:S(2)}, u32[]{:S(2)}) %all-to-all-start.3) | async-done | bytes 3932192 | tf_op jit(solution)/shard_map/all_to_all | solution.py:95
  318.1 9.8 %all-to-all-start.1 = ((bf16[32,36,2560]{2,1,0:T(8,128)(2,1)}), bf16[32,36,2560]{2,1,0:T(8,128)(2,1)}, u32[]{:S(2)}, u32[]{:S(2)}) async-start(bf16[32,36,2560]{2,1,0:T(8,128)(2,1)} %reshape.170), calls=%async_computation.1 | async-start | bytes 13107200 | tf_op jit(solution)/shard_map/all_to_all | solution.py:114
  328.0 0.0 copy-start.4
  328.0 0.0 all-gather.4.cloned.1.call-start
  328.0 0.0 copy-done.2
  328.0 1.1 copy.83
  329.1 0.3 copy.84
  329.4 0.3 copy.90
  330.4 4.2 mul.99
  334.6 9.2 %copy.88 = f32[8,320,768]{2,1,0:T(8,128)} copy(f32[8,320,768]{1,2,0:T(8,128)} %bitcast.55) | data formatting | bytes 15728640 | tf_op jit(solution)/shard_map/mul | solution.py:107
  343.8 5.3 %multiply_reduce_fusion = f32[320,768]{1,0:T(8,128)S(1)} fusion(f32[8,320,768]{2,1,0:T(8,128)} %copy.88, bf16[8,320,768]{2,1,0:T(8,128)(2,1)} %all-to-all-done.3), kind=kLoop, calls=%fused_computation.5 | loop fusion | flops 5652480 | bytes 12779520 | tf_op jit(solution)/shard_map/reduce_sum | solution.py:106
  349.1 0.4 copy.94
  349.5 2.2 fusion.7
  351.7 1.0 copy.91
  352.7 0.0 all-gather.4.cloned.1.call-update
  352.7 1.3 fusion.14
  354.0 2.1 copy.92
  356.1 1.0 copy.93
  357.1 116.8 %all-to-all-done.1 = bf16[32,36,2560]{2,1,0:T(8,128)(2,1)} async-done(((bf16[32,36,2560]{2,1,0:T(8,128)(2,1)}), bf16[32,36,2560]{2,1,0:T(8,128)(2,1)}, u32[]{:S(2)}, u32[]{:S(2)}) %all-to-all-start.1) | async-done | bytes 5898272 | tf_op jit(solution)/shard_map/all_to_all | solution.py:114
  473.9 8.1 %reshape.171 = bf16[1152,2560]{1,0:T(8,128)(2,1)} reshape(bf16[32,36,2560]{2,1,0:T(8,128)(2,1)} %all-to-all-done.1) | data formatting | bytes 11796480 | tf_op jit(solution)/shard_map/reshape | solution.py:117
  482.0 11.8 %gather_fusion = bf16[768,2560]{1,0:T(8,128)(2,1)} fusion(bf16[1152,2560]{1,0:T(8,128)(2,1)} %reshape.171, s32[1024]{0:T(1024)S(1)} %pad_clamp_fusion.1), kind=kCustom, calls=%fused_computation | custom fusion | bytes 7867392 | tf_op jit(solution)/shard_map/gather | solution.py:117
  493.8 7.1 %reshape.173 = bf16[128,6,2560]{2,1,0:T(8,128)(2,1)} reshape(bf16[768,2560]{1,0:T(8,128)(2,1)} %gather_fusion) | data formatting | bytes 7864320 | tf_op jit(solution)/shard_map/reshape | solution.py:117
  500.9 6.5 %reduce_sum.44 = bf16[128,2560]{1,0:T(8,128)(2,1)} reduce(bf16[128,6,2560]{2,1,0:T(8,128)(2,1)} %reshape.173, bf16[]{:T(256)} %constant.11.clone.1), dimensions={1}, to_apply=%region_4.5 | reduce | flops 1638400 | bytes 4587522 | tf_op jit(solution)/shard_map/reduce_sum | solution.py:118
  507.4 4.4 copy.99
  511.8 0.0 copy-done.1
  (18 shorter events, 0.1 us)
Async XLA Ops:
  7.2 20.3 %copy-start = (bf16[128,2560]{1,0:T(8,128)(2,1)S(1)}, bf16[128,2560]{1,0:T(8,128)(2,1)}, u32[]{:S(2)}) copy-start(bf16[128,2560]{1,0:T(8,128)(2,1)} %param.8) | copy-start | bytes 1966084
  11.2 30.6 %all-to-all-start = ((bf16[32,1,1]{2,1,0:T(2,128)(2,1)}), bf16[32,1,1]{2,1,0:T(2,128)(2,1)S(1)}, u32[]{:S(2)}, u32[]{:S(2)}) async-start(bf16[32,1,1]{2,1,0:T(2,128)(2,1)} %copy.79), calls=%async_computation | async-start | bytes 32768 | tf_op jit(solution)/shard_map/all_to_all | solution.py:75
  41.9 153.8 %all-to-all-start.2 = ((bf16[32,36,2560]{2,1,0:T(8,128)(2,1)}), bf16[32,36,2560]{2,1,0:T(8,128)(2,1)}, u32[]{:S(2)}, u32[]{:S(2)}) async-start(bf16[32,36,2560]{2,1,0:T(8,128)(2,1)} %reshape.174), calls=%async_computation.2 | async-start | bytes 13107200 | tf_op jit(solution)/shard_map/all_to_all | solution.py:74
  51.2 220.9 %all-gather.6.cloned.1.call-start = ((), (), s32[]{:S(2)}) async-start(), calls=%async_computation.6 | async-start | bytes 4423680 | tf_op jit(solution)/shard_map/all_gather | solution.py:87
  52.8 151.0 %copy-start.5 = (bf16[1,1152,768]{2,1,0:T(8,128)(2,1)S(1)}, bf16[1,1152,768]{2,1,0:T(8,128)(2,1)}, u32[]{:S(2)}) copy-start(bf16[1,1152,768]{2,1,0:T(8,128)(2,1)} %param.10) | copy-start | bytes 5308420
  252.9 14.4 %all-to-all-start.4 = ((bf16[8,320,6]{1,2,0:T(8,128)(2,1)}), bf16[8,320,6]{1,2,0:T(8,128)(2,1)S(1)}, u32[]{:S(2)}, u32[]{:S(2)}) async-start(bf16[8,320,6]{1,2,0:T(8,128)(2,1)} %copy.87), calls=%async_computation.4 | async-start | bytes 98304 | tf_op jit(solution)/shard_map/all_to_all | solution.py:98
  267.4 50.8 %all-to-all-start.3 = ((bf16[8,320,768]{2,1,0:T(8,128)(2,1)}), bf16[8,320,768]{2,1,0:T(8,128)(2,1)}, u32[]{:S(2)}, u32[]{:S(2)}) async-start(bf16[8,320,768]{2,1,0:T(8,128)(2,1)} %divide_convert_fusion), calls=%async_computation.3 | async-start | bytes 7864320 | tf_op jit(solution)/shard_map/all_to_all | solution.py:95
  289.3 38.7 %copy-start.2 = (bf16[1,320,768]{2,1,0:T(8,128)(2,1)S(1)}, bf16[1,320,768]{2,1,0:T(8,128)(2,1)}, u32[]{:S(2)}) copy-start(bf16[1,320,768]{2,1,0:T(8,128)(2,1)} %param.11) | copy-start | bytes 1474564
  289.3 39.8 %copy-start.3 = (bf16[1,320,768]{2,1,0:T(8,128)(2,1)S(1)}, bf16[1,320,768]{2,1,0:T(8,128)(2,1)}, u32[]{:S(2)}) copy-start(bf16[1,320,768]{2,1,0:T(8,128)(2,1)} %param.13) | copy-start | bytes 1474564
  318.1 155.7 %all-to-all-start.1 = ((bf16[32,36,2560]{2,1,0:T(8,128)(2,1)}), bf16[32,36,2560]{2,1,0:T(8,128)(2,1)}, u32[]{:S(2)}, u32[]{:S(2)}) async-start(bf16[32,36,2560]{2,1,0:T(8,128)(2,1)} %reshape.170), calls=%async_computation.1 | async-start | bytes 13107200 | tf_op jit(solution)/shard_map/all_to_all | solution.py:114
  328.0 1.4 copy-start.4
  328.0 179.4 %all-gather.4.cloned.1.call-start = ((), (), s32[]{:S(2)}) async-start(), calls=%async_computation.5 | async-start | bytes 4423680 | tf_op jit(solution)/shard_map/all_gather | solution.py:113
  507.4 4.4 copy-start.1
Sparse Core Ops, SparseCore 0:
  53.9 36.1 all-gather.5
  352.8 33.8 all-gather.3
where the time goes:
time: 521 us; the launch traced here: 519 us
  waiting for transfers between devices  289 us (55%)
  local copies, waits for them, and re-layouts  121 us (23%)
  starting transfers between devices  41.8 us (8%)
  other arithmetic  31.1 us (6%)
  matrix products  21.2 us (4%)
  between operations  14.9 us (3%)
    all_to_all x1, waiting for transfers between devices, on_device(): lax.all_to_all(outgoing, 'expert', split_axis=0, concat_axis=0, tiled=True)  143 us
    all_to_all x1, waiting for transfers between devices, on_device(): lax.all_to_all(returned.reshape(experts, capacity, D), 'expert', split_ax...  117 us
    all_to_all x1, waiting for transfers between devices, on_device(): lax.all_to_all(levels.reshape(copies, shard_rows, FF), 'dp', split_axis=0...  28.8 us
    div x3, local copies, waits for them, and re-layouts, dequantized(): blocks / block_scale.astype(jnp.float32)[:, :, None]  23.2 us
    reshape x2, local copies, waits for them, and re-layouts, on_device(): picked = came_back.reshape(slot_count, D)[target].reshape(TOK_DEV, TOP, D)  15.3 us
    mul x2, local copies, waits for them, and re-layouts, on_device(): got_levels.astype(jnp.float32).reshape(copies, shard_rows, FF // QB, QB)  13.4 us
    dot_general x1, matrix products, on_device(): lax.dot_general(arrived_rows, masked, (((0,), (0,)), ((), ())), preferred...  12.2 us
    all_to_all x1, starting transfers between devices, on_device(): lax.all_to_all(count_values, 'expert', split_axis=0, concat_axis=0, tiled...  11.9 us
  transfers between devices with their start and end apart: 7, of which 3 were waited for; matrix products, arithmetic and copies ran while one was open for 32% of the time, Pallas kernels for 0%

commit v1 on v0

v1 whole, which is shorter than its diff:
```python
import jax
import jax.numpy as jnp
from jax import lax
from jax.experimental import pallas as pl
from jax.experimental.pallas import tpu as pltpu
from jax.sharding import Mesh, PartitionSpec as P

D = 2560
FF = 768
TOP = 6
QB = 128
NQ = FF // QB
STEP = 20
TOK = 128
CAP = 36
NX = 4
NZ = 8
NDP = 8
SHARD = D // NDP
INFO = 128
EXT = D + INFO
MSG = SHARD + 16
TILE = 512

learn_rate = 0.001
beta_one = 0.9
beta_two = 0.999
decay_rate = 0.1
adam_eps = 1e-08
quant_top = 127.0
amax_eps = 1e-06

CHUNKS = ((0, -1, 1), (-2, 2), (-3, 3, 4))
ROWS = tuple(-(-len(c) * CAP // 16) * 16 for c in CHUNKS)
bf16 = jnp.bfloat16
f32 = jnp.float32


def params(n=1):
    return pltpu.CompilerParams(dimension_semantics=("arbitrary",) * n)


def prep_kernel(routing_ref, tokens_ref, ext_ref):
    r = routing_ref[...]
    lane = lax.broadcasted_iota(jnp.int32, (TOK, INFO), 1)
    row = lax.broadcasted_iota(jnp.int32, (TOK, INFO), 0)
    named = jnp.zeros((TOK, INFO), f32)
    for k in range(TOP):
        named = named + jnp.where(r[:, k : k + 1] == lane, 1.0, 0.0)
    earlier = jnp.where(row > lane, 1.0, 0.0).astype(bf16)
    before = jnp.dot(earlier, named.astype(bf16), preferred_element_type=f32)
    info = jnp.zeros((TOK, INFO), f32)
    for k in range(TOP):
        e = r[:, k : k + 1]
        w = jnp.sum(jnp.where(e == lane, before, 0.0), axis=1, keepdims=True)
        info = info + jnp.where(lane == k, e.astype(f32), 0.0)
        info = info + jnp.where(lane == TOP + k, w, 0.0)
    ext_ref[:, :D] = tokens_ref[...]
    ext_ref[:, D:] = info.astype(bf16)


def prep(routing, tokens):
    return pl.pallas_call(
        prep_kernel,
        out_shape=jax.ShapeDtypeStruct((TOK, EXT), bf16),
        name="prep",
    )(routing, tokens)


def joined(refs):
    parts = [ref[...] for ref in refs]
    return parts[0] if len(parts) == 1 else jnp.concatenate(parts, axis=0)


def slot_of(e, w, x, z):
    ex = jnp.floor(e * 0.125)
    ez = e - ex * 8.0
    dx = ex - x
    dx = jnp.where(dx < 0.0, dx + float(NX), dx)
    return jnp.where(ez == z, dx * 64.0 + w, -1.0)


def dispatch(me, blocks, rows):
    nb = len(blocks)
    flat = [a for b in blocks for a in b]
    sizes = [len(b) for b in blocks]
    nf = len(flat)

    def kernel(me_ref, *refs):
        tok, inf, outs, hot = refs[:nf], refs[nf : 2 * nf], refs[2 * nf : 2 * nf + NX], refs[-1]

        @pl.when(pl.program_id(0) == 0)
        def _():
            x = me_ref[0].astype(f32)
            z = me_ref[1].astype(f32)
            row = lax.broadcasted_iota(jnp.int32, (rows, TOK), 0).astype(f32)
            at = 0
            for b in range(nb):
                info = jnp.transpose(joined(inf[at : at + sizes[b]]).astype(f32))
                at += sizes[b]
                code = slot_of(info[0:TOP], info[TOP : 2 * TOP], x, z)
                for dx in range(NX):
                    want = jnp.where(
                        (row >= float(CAP * b)) & (row < float(CAP * (b + 1))),
                        row - float(CAP * b) + 64.0 * dx,
                        -2.0,
                    )
                    hit = jnp.zeros((rows, TOK), f32)
                    for k in range(TOP):
                        hit = jnp.where(want == code[k : k + 1, :], 1.0, hit)
                    hot[dx, :, b * TOK : (b + 1) * TOK] = hit.astype(bf16)

        at = 0
        values = []
        for b in range(nb):
            values.append(joined(tok[at : at + sizes[b]]))
            at += sizes[b]
        t = values[0] if nb == 1 else jnp.concatenate(values, axis=0)
        for dx in range(NX):
            outs[dx][...] = jnp.dot(hot[dx], t, preferred_element_type=f32).astype(bf16)

    specs = [pl.BlockSpec((a.shape[0], TILE), lambda i, m: (0, i)) for a in flat]
    specs += [pl.BlockSpec((a.shape[0], INFO), lambda i, m: (0, D // INFO)) for a in flat]
    return pl.pallas_call(
        kernel,
        out_shape=[jax.ShapeDtypeStruct((rows, D), bf16)] * NX,
        grid_spec=pltpu.PrefetchScalarGridSpec(
            num_scalar_prefetch=1,
            grid=(D // TILE,),
            in_specs=specs,
            out_specs=[pl.BlockSpec((rows, TILE), lambda i, m: (0, i))] * NX,
            scratch_shapes=[pltpu.VMEM((NX, rows, nb * TOK), bf16)],
        ),
        compiler_params=params(),
        name="dispatch",
    )(me, *flat, *flat)


def combine(me, rows_in, parts, slots, adds):
    rows = rows_in[0].shape[0]
    nb = len(parts)
    flat = [a for p in parts for a in p]
    sizes = [len(p) for p in parts]
    nf = len(flat)
    added = [a for p in adds for a, _ in p]
    na = len(added)

    def kernel(me_ref, *refs):
        src, inf = refs[:NX], refs[NX : NX + nf]
        extra = refs[NX + nf : NX + nf + na]
        outs = refs[NX + nf + na : NX + nf + na + nb]
        hot = refs[-1]

        @pl.when(pl.program_id(0) == 0)
        def _():
            x = me_ref[0].astype(f32)
            z = me_ref[1].astype(f32)
            lane = lax.broadcasted_iota(jnp.int32, (TOK, rows), 1).astype(f32)
            at = 0
            for b in range(nb):
                info = joined(inf[at : at + sizes[b]]).astype(f32)
                at += sizes[b]
                code = slot_of(info[:, 0:TOP], info[:, TOP : 2 * TOP], x, z)
                first = CAP * slots[b]
                for dx in range(NX):
                    want = jnp.where(
                        (lane >= float(first)) & (lane < float(first + CAP)),
                        lane - float(first) + 64.0 * dx,
                        -2.0,
                    )
                    hit = jnp.zeros((TOK, rows), f32)
                    for k in range(TOP):
                        hit = jnp.where(want == code[:, k : k + 1], 1.0, hit)
                    hot[dx, b * TOK : (b + 1) * TOK, :] = hit.astype(bf16)

        total = jnp.dot(hot[0], src[0][...], preferred_element_type=f32)
        for dx in range(1, NX):
            total = total + jnp.dot(hot[dx], src[dx][...], preferred_element_type=f32)
        at = 0
        for b in range(nb):
            mine = total[b * TOK : (b + 1) * TOK]
            for _, (first, count) in adds[b]:
                more = extra[at][...].astype(f32)
                at += 1
                if count < TOK:
                    pad = jnp.zeros((TOK - count, TILE), f32)
                    more = jnp.concatenate([more, pad] if first == 0 else [pad, more], axis=0)
                mine = mine + more
            outs[b][...] = mine.astype(bf16)

    specs = [pl.BlockSpec((rows, TILE), lambda i, m: (0, i))] * NX
    specs += [pl.BlockSpec((a.shape[0], INFO), lambda i, m: (0, D // INFO)) for a in flat]
    specs += [pl.BlockSpec((a.shape[0], TILE), lambda i, m: (0, i)) for a in added]
    return pl.pallas_call(
        kernel,
        out_shape=[jax.ShapeDtypeStruct((TOK, D), bf16)] * nb,
        grid_spec=pltpu.PrefetchScalarGridSpec(
            num_scalar_prefetch=1,
            grid=(D // TILE,),
            in_specs=specs,
            out_specs=[pl.BlockSpec((TOK, TILE), lambda i, m: (0, i))] * nb,
            scratch_shapes=[pltpu.VMEM((NX, nb * TOK, rows), bf16)],
        ),
        compiler_params=params(),
        name="combine",
    )(me, *rows_in, *flat, *added)


def order_kernel(me_ref, up_ref, *outs):
    x, z = me_ref[0], me_ref[1]
    for c, offsets in enumerate(CHUNKS):
        rows = ROWS[c]
        row = lax.broadcasted_iota(jnp.int32, (rows, NZ * CAP), 0)
        col = lax.broadcasted_iota(jnp.int32, (rows, NZ * CAP), 1)
        want = jnp.full((rows, NZ * CAP), -1, jnp.int32)
        for b, offset in enumerate(offsets):
            block = lax.rem(z + offset + NZ, NZ)
            inside = (row >= CAP * b) & (row < CAP * (b + 1))
            want = jnp.where(inside, block * CAP + row - CAP * b, want)
        pick = jnp.where(want == col, 1.0, 0.0).astype(bf16)
        for dx in range(NX):
            source = lax.rem(x - dx + NX, NX)
            start = pl.multiple_of(source * (NZ * CAP), 16)
            part = up_ref[pl.ds(start, NZ * CAP), :]
            outs[c][dx * rows : (dx + 1) * rows, :] = jnp.dot(
                pick, part, preferred_element_type=f32
            ).astype(bf16)


def ordered(me, up):
    return pl.pallas_call(
        order_kernel,
        out_shape=[jax.ShapeDtypeStruct((NX * r, FF), bf16) for r in ROWS],
        in_specs=[
            pl.BlockSpec(memory_space=pltpu.SMEM),
            pl.BlockSpec(memory_space=pltpu.VMEM),
        ],
        out_specs=[pl.BlockSpec(memory_space=pltpu.VMEM)] * len(ROWS),
        name="order",
    )(me, up)


def slot_grads(ups, weights):
    nc = len(ups)

    def kernel(*refs):
        up, w, outs = refs[:nc], refs[nc], refs[nc + 1 :]
        for c in range(nc):
            for dx in range(NX):
                r = ROWS[c]
                outs[c * NX + dx][...] = lax.dot_general(
                    up[c][dx * r : (dx + 1) * r, :],
                    w[...],
                    (((1,), (1,)), ((), ())),
                    preferred_element_type=f32,
                ).astype(bf16)

    flat_rows = [r for r in ROWS for _ in range(NX)]
    out = pl.pallas_call(
        kernel,
        out_shape=[jax.ShapeDtypeStruct((r, D), bf16) for r in flat_rows],
        grid=(D // TILE,),
        in_specs=[pl.BlockSpec((NX * r, FF), lambda i: (0, 0)) for r in ROWS]
        + [pl.BlockSpec((TILE, FF), lambda i: (i, 0))],
        out_specs=[pl.BlockSpec((r, TILE), lambda i: (0, i)) for r in flat_rows],
        compiler_params=params(),
        name="slot_grads",
    )(*ups, weights)
    return [out[c * NX : (c + 1) * NX] for c in range(nc)]


def levels_of(rows_in, ups, error):
    flat = [a for c in rows_in for a in c]
    nc = len(rows_in)
    wide = 2 * SHARD

    def kernel(*refs):
        src, up, err, out = refs[: len(flat)], refs[len(flat) : len(flat) + nc], refs[-2], refs[-1]
        total = err[...].astype(f32)
        for c in range(nc):
            slab = jnp.concatenate([src[c * NX + dx][...] for dx in range(NX)], axis=0)
            total = total + lax.dot_general(
                slab, up[c][...], (((0,), (0,)), ((), ())), preferred_element_type=f32
            )
        lane = lax.broadcasted_iota(jnp.int32, (wide, QB), 1)
        scales = jnp.zeros((wide, QB), f32)
        for q in range(NQ):
            block = total[:, q * QB : (q + 1) * QB]
            top = jnp.max(jnp.abs(block), axis=1, keepdims=True)
            scale = ((top + amax_eps) / quant_top).astype(bf16).astype(f32)
            level = (block * (1.0 / scale)).astype(bf16)
            out[0, :SHARD, q * QB : (q + 1) * QB] = level[:SHARD]
            out[1, :SHARD, q * QB : (q + 1) * QB] = level[SHARD:]
            scales = jnp.where(lane == q, scale, scales)
        for h in range(2):
            flipped = jnp.transpose(scales[h * SHARD : (h + 1) * SHARD])[:16]
            pad = jnp.zeros((16, FF - SHARD), f32)
            out[h, SHARD:, :] = jnp.concatenate([flipped, pad], axis=1).astype(bf16)

    return pl.pallas_call(
        kernel,
        out_shape=jax.ShapeDtypeStruct((NDP, MSG, FF), bf16),
        grid=(D // wide,),
        in_specs=[pl.BlockSpec((a.shape[0], wide), lambda i: (0, i)) for a in flat]
        + [pl.BlockSpec((NX * r, FF), lambda i: (0, 0)) for r in ROWS]
        + [pl.BlockSpec((wide, FF), lambda i: (i, 0))],
        out_specs=pl.BlockSpec((2, MSG, FF), lambda i: (i, 0, 0)),
        compiler_params=params(),
        name="levels",
    )(*flat, *ups, error)


def adam_kernel(loss_ref, got_ref, scale_ref, w_ref, m_ref, v_ref, nw_ref, nm_ref, nv_ref, sc_ref):
    q = pl.program_id(0)

    @pl.when(q == 0)
    def _():
        for d in range(NDP):
            sc_ref[:, d, :] = scale_ref[d].astype(f32)[:, :384]

    scales = jnp.transpose(sc_ref[q])
    total = jnp.zeros((SHARD, QB), f32)
    for d in range(NDP):
        total = total + got_ref[d].astype(f32) * scales[:SHARD, d : d + 1]
    gradient = total / loss_ref[0]
    first = beta_one * m_ref[...].astype(f32) + (1.0 - beta_one) * gradient
    second = beta_two * v_ref[...].astype(f32) + (1.0 - beta_two) * gradient * gradient
    first_hat = first / (1.0 - beta_one**STEP)
    second_hat = second / (1.0 - beta_two**STEP)
    master = w_ref[...].astype(f32)
    updated = master - learn_rate * (
        first_hat / (jnp.sqrt(second_hat) + adam_eps) + decay_rate * master
    )
    nw_ref[...] = updated.astype(bf16)
    nm_ref[...] = first.astype(bf16)
    nv_ref[...] = second.astype(bf16)


def adam(loss, got, w, m, v):
    column = pl.BlockSpec((SHARD, QB), lambda i: (0, i))
    return pl.pallas_call(
        adam_kernel,
        out_shape=[jax.ShapeDtypeStruct((SHARD, FF), bf16)] * 3,
        grid=(NQ,),
        in_specs=[
            pl.BlockSpec(memory_space=pltpu.SMEM),
            pl.BlockSpec((NDP, SHARD, QB), lambda i: (0, 0, i)),
            pl.BlockSpec((NDP, 16, FF), lambda i: (0, SHARD // 16, 0)),
            column,
            column,
            column,
        ],
        out_specs=[column] * 3,
        scratch_shapes=[pltpu.VMEM((16, NDP, 384), f32)],
        compiler_params=params(),
        name="adam",
    )(loss, got, got, w, m, v)


def on_device(tokens, routing, grad_up, up_shard, error_feedback, moment_one, moment_two, loss):
    def along(axis, n, shift):
        return lambda a: lax.ppermute(a, axis, [(i, (i + shift) % n) for i in range(n)])

    up_z, down_z = along("z", NZ, 1), along("z", NZ, -1)
    me = jnp.stack([lax.axis_index("x"), lax.axis_index("z")]).astype(jnp.int32)
    weights = lax.all_gather(up_shard[0], "dp", axis=0, tiled=True)

    ext = prep(routing, tokens)
    block = {0: [ext]}
    up, down = ext, ext
    for r in (1, 2, 3):
        up, down = up_z(up), down_z(down)
        block[-r], block[r] = [up], [down]
    block[4] = [up_z(up[: TOK // 2]), down_z(down[TOK // 2 :])]

    arrived = []
    for offsets, rows in zip(CHUNKS, ROWS):
        out = dispatch(me, [block[o] for o in offsets], rows)
        arrived.append([out[0]] + [along("x", NX, dx)(out[dx]) for dx in range(1, NX)])

    ups = ordered(me, grad_up[0])
    packed = levels_of(arrived, ups, error_feedback[0])
    got = lax.all_to_all(packed, "dp", split_axis=0, concat_axis=0, tiled=True)
    new_w, new_m, new_v = adam(
        loss.reshape(1), got, up_shard[0], moment_one[0], moment_two[0]
    )
    full = lax.all_gather(new_w, "dp", axis=0, tiled=True)

    returned = slot_grads(ups, weights)
    back = [None] * len(CHUNKS)
    for c in reversed(range(len(CHUNKS))):
        out = returned[c]
        back[c] = [out[0]] + [along("x", NX, -dx)(out[dx]) for dx in range(1, NX)]
    half = TOK // 2
    (far,) = combine(me, back[2], [block[4]], [2], [[]])
    fwd, bwd = up_z(far[:half]), down_z(far[half:])
    top, low = (0, half), (half, half)
    whole = (0, TOK)
    q_up, q_down = combine(
        me, back[2], [block[3], block[-3]], [1, 0], [[(fwd, top)], [(bwd, low)]]
    )
    q_up, q_down = up_z(q_up), down_z(q_down)
    q_up, q_down = combine(
        me, back[1], [block[2], block[-2]], [1, 0], [[(q_up, whole)], [(q_down, whole)]]
    )
    q_up, q_down = up_z(q_up), down_z(q_down)
    q_up, q_down = combine(
        me, back[0], [block[1], block[-1]], [2, 1], [[(q_up, whole)], [(q_down, whole)]]
    )
    q_up, q_down = up_z(q_up), down_z(q_down)
    (grad_tokens,) = combine(
        me, back[0], [block[0]], [0], [[(q_up, whole), (q_down, whole)]]
    )
    return (grad_tokens, full[None], new_m[None], new_v[None])


def solution(mesh):
    fine = Mesh(mesh.devices.reshape(NX, NZ, NDP), ("x", "z", "dp"))
    expert = ("x", "z")
    in_specs = (
        P(("x", "z", "dp"), None),
        P(("x", "z", "dp"), None),
        P(expert, "dp", None),
        P(expert, "dp", None),
        P(expert, "dp", None),
        P(expert, "dp", None),
        P(expert, "dp", None),
        P(),
    )
    out_specs = (
        P(("x", "z", "dp"), None),
        P(expert, None, None),
        P(expert, "dp", None),
        P(expert, "dp", None),
    )
    return jax.shard_map(
        on_device, mesh=fine, in_specs=in_specs, out_specs=out_specs, check_vma=False
    )
```

time: 521 us -> 404 us (0.78)
  local copies, waits for them, and re-layouts: 121 us -> 16.1 us
  Pallas kernels: 0 us -> 94.3 us
  waiting for transfers between devices: 289 us -> 229 us
  other arithmetic: 31.1 us -> 0.61 us
  matrix products: 21.2 us -> 0 us
  starting transfers between devices: 41.8 us -> 48.2 us
    all_to_all x5 -> x1, waiting for transfers between devices: 288 us -> 47.4 us  [on_device(): got = lax.all_to_all(packed, 'dp', split_axis=0, concat_axis=0, tiled=True)]
    ppermute x0 -> x34, waiting for transfers between devices: none -> 181 us  [along(): lax.ppermute(a, axis, [(i, (i + shift) % n) for i in range(n)])]
    pallas_call x0 -> x13, Pallas kernels: none -> 94.3 us  [the longest x5 31.9 us: combine(): pl.pallas_call(kernel, out_shape=[jax.ShapeDtypeStruct((TOK, D), bf16)] *...]
    ppermute x0 -> x34, starting transfers between devices: none -> 41.5 us  [along(): lax.ppermute(a, axis, [(i, (i + shift) % n) for i in range(n)])]
    reshape x5 -> x0, local copies, waits for them, and re-layouts: 39.5 us -> none  [the longest x2 15.3 us: on_device(): picked = came_back.reshape(slot_count, D)[target].reshape(TOK_DEV, TOP, D)]
    all_to_all x5 -> x1, starting transfers between devices: 41.7 us -> 6.64 us  [on_device(): got = lax.all_to_all(packed, 'dp', split_axis=0, concat_axis=0, tiled=True)]
    div x3 -> x0, local copies, waits for them, and re-layouts: 23.2 us -> none  [dequantized(): blocks / block_scale.astype(jnp.float32)[:, :, None]]
    dot_general x2 -> x0, matrix products: 21.2 us -> none  [the longest x1 12.2 us: on_device(): lax.dot_general(arrived_rows, masked, (((0,), (0,)), ((), ())), preferred...]
  transfers between devices with their start and end apart: 7 -> 37, of which waited for: 3 -> 20; matrix products, arithmetic and copies ran while one was open for 32% -> 1% of each run, Pallas kernels for 0% -> 23%
where the time goes in v1:
time: 404 us; the launch traced here: 403 us
  waiting for transfers between devices  229 us (57%)
  Pallas kernels  94.3 us (23%)
  starting transfers between devices  48.2 us (12%)
  local copies, waits for them, and re-layouts  16.1 us (4%)
  between operations  14.9 us (4%)
    ppermute x34, waiting for transfers between devices, along(): lax.ppermute(a, axis, [(i, (i + shift) % n) for i in range(n)])  181 us
    all_to_all x1, waiting for transfers between devices, on_device(): got = lax.all_to_all(packed, 'dp', split_axis=0, concat_axis=0, tiled=True)  47.4 us
    ppermute x34, starting transfers between devices, along(): lax.ppermute(a, axis, [(i, (i + shift) % n) for i in range(n)])  41.5 us
    pallas_call x5, Pallas kernels, combine(): pl.pallas_call(kernel, out_shape=[jax.ShapeDtypeStruct((TOK, D), bf16)] *...  31.9 us
    pallas_call x3, Pallas kernels, dispatch(): pl.pallas_call(kernel, out_shape=[jax.ShapeDtypeStruct((rows, D), bf16)]...  18.2 us
    pallas_call x1, Pallas kernels, slot_grads(): pl.pallas_call(kernel, out_shape=[jax.ShapeDtypeStruct((r, D), bf16) for...  17.6 us
    unnamed x66, local copies, waits for them, and re-layouts  14.1 us
    pallas_call x1, Pallas kernels, levels_of(): pl.pallas_call(kernel, out_shape=jax.ShapeDtypeStruct((NDP, MSG, FF), bf1...  12.6 us
  transfers between devices with their start and end apart: 37, of which 20 were waited for; matrix products, arithmetic and copies ran while one was open for 1% of the time, Pallas kernels for 23%

profile of v1, /device:TPU:1, one launch (start us, length us, event | category | flops | bytes accessed | tf_op | source)
XLA Modules:
  0.0 402.8 jit_solution(4963052709908343790)
XLA Ops:
  7.2 1.4 copy.12.routing_ref
  8.6 2.7 prep.1.refs_4_.refs_0_.refs_3_
  11.3 2.5 collective-permute-start.4
  13.8 4.0 collective-permute-start.3
  17.8 15.2 %collective-permute-done.4.refs_5_.refs_1_.refs_4_ = bf16[128,2688]{1,0:T(8,128)(2,1)S(1)} collective-permute-done((bf16[128,2688]{1,0:T(8,128)(2,1)}, bf16[128,2688]{1,0:T(8,128)(2,1)S(1)}, u32[]{:S(2)}, u32[]{:S(2)}) %collective-permute-start.4) | collective-permute-done | bytes 688160 | tf_op jit(solution)/shard_map/ppermute | solution.py:362
  33.1 2.7 collective-permute-start.8
  35.7 14.3 %collective-permute-done.9.refs_5_.refs_0_.refs_2_ = bf16[128,2688]{1,0:T(8,128)(2,1)S(1)} collective-permute-done((bf16[128,2688]{1,0:T(8,128)(2,1)S(1)}, bf16[128,2688]{1,0:T(8,128)(2,1)S(1)}, u32[]{:S(2)}, u32[]{:S(2)}) %collective-permute-start.9) | collective-permute-done | bytes 688160 | tf_op jit(solution)/shard_map/ppermute | solution.py:362
  50.0 2.7 collective-permute-start.13
  52.8 13.3 %collective-permute-done.14.refs_5_.refs_0_.refs_4_ = bf16[128,2688]{1,0:T(8,128)(2,1)S(1)} collective-permute-done((bf16[128,2688]{1,0:T(8,128)(2,1)S(1)}, bf16[128,2688]{1,0:T(8,128)(2,1)S(1)}, u32[]{:S(2)}, u32[]{:S(2)}) %collective-permute-start.14) | collective-permute-done | bytes 688160 | tf_op jit(solution)/shard_map/ppermute | solution.py:362
  66.1 0.8 slice.16
  67.5 6.3 %dispatch.3 = (bf16[112,2560]{1,0:T(8,128)(2,1)}, bf16[112,2560]{1,0:T(8,128)(2,1)}, bf16[112,2560]{1,0:T(8,128)(2,1)}, bf16[112,2560]{1,0:T(8,128)(2,1)}) custom-call(s32[2]{0:T(128)} %pad_add_fusion.me_ref, bf16[128,2688]{1,0:T(8,128)(2,1)} %prep.1.refs_4_.refs_0_.refs_3_, bf16[128,2688]{1,0:T(8,128)(2,1)} %copy-done.4, bf16[128,2688]{1,0:T(8,128)(2,1)} %copy-done.5, ...), custom_call_target="tpu_custom_call" | custom-call | tf_op jit(solution)/shard_map/dispatch/pallas_call | solution.py:124
  73.8 1.2 collective-permute-start.25
  75.1 2.5 collective-permute-start.26
  77.5 1.2 collective-permute-start.27
  78.7 2.7 collective-permute-start.16
  81.5 5.6 %dispatch.4 = (bf16[80,2560]{1,0:T(8,128)(2,1)}, bf16[80,2560]{1,0:T(8,128)(2,1)}, bf16[80,2560]{1,0:T(8,128)(2,1)}, bf16[80,2560]{1,0:T(8,128)(2,1)}) custom-call(s32[2]{0:T(128)} %pad_add_fusion.me_ref, bf16[128,2688]{1,0:T(8,128)(2,1)} %copy-done.2, bf16[128,2688]{1,0:T(8,128)(2,1)} %copy-done.3, bf16[128,2688]{1,0:T(8,128)(2,1)} %copy-done.2, ...), custom_call_target="tpu_custom_call" | custom-call | tf_op jit(solution)/shard_map/dispatch/pallas_call | solution.py:124
  87.4 0.7 copy-done.6
  88.2 6.3 %dispatch.5 = (bf16[112,2560]{1,0:T(8,128)(2,1)}, bf16[112,2560]{1,0:T(8,128)(2,1)}, bf16[112,2560]{1,0:T(8,128)(2,1)}, bf16[112,2560]{1,0:T(8,128)(2,1)}) custom-call(s32[2]{0:T(128)} %pad_add_fusion.me_ref, bf16[128,2688]{1,0:T(8,128)(2,1)} %copy-done, bf16[128,2688]{1,0:T(8,128)(2,1)} %copy-done.1, ...), custom_call_target="tpu_custom_call" | custom-call | tf_op jit(solution)/shard_map/dispatch/pallas_call | solution.py:124
  94.7 3.5 collective-permute-start.32
  98.2 2.0 collective-permute-done.26.refs_2_
  100.3 4.9 %collective-permute-done.27.refs_3_ = bf16[112,2560]{1,0:T(8,128)(2,1)} collective-permute-done((bf16[112,2560]{1,0:T(8,128)(2,1)}, bf16[112,2560]{1,0:T(8,128)(2,1)}, u32[]{:S(2)}, u32[]{:S(2)}) %collective-permute-start.27) | collective-permute-done | bytes 573472 | tf_op jit(solution)/shard_map/ppermute | solution.py:362
  105.2 5.1 %collective-permute-done.28.refs_5_ = bf16[80,2560]{1,0:T(8,128)(2,1)S(1)} collective-permute-done((bf16[80,2560]{1,0:T(8,128)(2,1)}, bf16[80,2560]{1,0:T(8,128)(2,1)S(1)}, u32[]{:S(2)}, u32[]{:S(2)}) %collective-permute-start.28) | collective-permute-done | bytes 409632 | tf_op jit(solution)/shard_map/ppermute | solution.py:362
  110.2 3.9 order.1
  114.2 28.1 %collective-permute-done.29.refs_6_ = bf16[80,2560]{1,0:T(8,128)(2,1)S(1)} collective-permute-done((bf16[80,2560]{1,0:T(8,128)(2,1)}, bf16[80,2560]{1,0:T(8,128)(2,1)S(1)}, u32[]{:S(2)}, u32[]{:S(2)}) %collective-permute-start.29) | collective-permute-done | bytes 409632 | tf_op jit(solution)/shard_map/ppermute | solution.py:362
  142.3 1.9 collective-permute-done.30.refs_7_
  145.6 12.6 %levels.1 = bf16[8,336,768]{2,1,0:T(8,128)(2,1)} custom-call(bf16[112,2560]{1,0:T(8,128)(2,1)} %get-tuple-element.61.refs_0_, bf16[112,2560]{1,0:T(8,128)(2,1)} %collective-permute-done.25.refs_1_, bf16[112,2560]{1,0:T(8,128)(2,1)} %collective-permute-done.26.refs_2_, bf16[112,2560]{1,0:T(8,128)(2,1)} %collective-permute-done.27.refs_3_, ...), custom_call_target="tpu_custom_call" | custom-call | tf_op jit(solution)/shard_map/levels/pallas_call | solution.py:300
  158.2 6.6 %all-to-all-start = ((bf16[8,336,768]{2,1,0:T(8,128)(2,1)}), bf16[8,336,768]{2,1,0:T(8,128)(2,1)}, u32[]{:S(2)}, u32[]{:S(2)}) async-start(bf16[8,336,768]{2,1,0:T(8,128)(2,1)} %levels.1), calls=%async_computation | async-start | bytes 8257536 | tf_op jit(solution)/shard_map/all_to_all | solution.py:383
  165.5 47.4 %all-to-all-done.got_ref.scale_ref = bf16[8,336,768]{2,1,0:T(8,128)(2,1)} async-done(((bf16[8,336,768]{2,1,0:T(8,128)(2,1)}), bf16[8,336,768]{2,1,0:T(8,128)(2,1)}, u32[]{:S(2)}, u32[]{:S(2)}) %all-to-all-start) | async-done | bytes 4128800 | tf_op jit(solution)/shard_map/all_to_all | solution.py:383
  212.9 7.5 %adam.1 = (bf16[320,768]{1,0:T(8,128)(2,1)}, bf16[320,768]{1,0:T(8,128)(2,1)}, bf16[320,768]{1,0:T(8,128)(2,1)}) custom-call(f32[1]{0:T(128)} %bitcast.12.loss_ref, bf16[8,336,768]{2,1,0:T(8,128)(2,1)} %all-to-all-done.got_ref.scale_ref, bf16[8,336,768]{2,1,0:T(8,128)(2,1)} %all-to-all-done.got_ref.scale_ref, bf16[320,768]{1,0:T(8,128)(2,1)} %bitcast.16, ...), custom_call_target="tpu_custom_call" | custom-call | tf_op jit(solution)/shard_map/adam/pallas_call | solution.py:341
  220.5 17.6 %slot_grads.1 = (bf16[112,2560]{1,0:T(8,128)(2,1)}, bf16[112,2560]{1,0:T(8,128)(2,1)}, bf16[112,2560]{1,0:T(8,128)(2,1)}, bf16[112,2560]{1,0:T(8,128)(2,1)}, bf1...) custom-call(bf16[448,768]{1,0:T(8,128)(2,1)} %get-tuple-element.40.r, ...), custom_call_target="tpu_custom_call" | custom-call | tf_op jit(solution)/shard_map/slot_grads/pallas_call | solution.py:259
  238.0 1.9 collective-permute-start.10
  239.9 0.9 collective-permute-start.11
  241.3 10.6 %collective-permute-done.10.refs_1_ = bf16[112,2560]{1,0:T(8,128)(2,1)S(1)} collective-permute-done((bf16[112,2560]{1,0:T(8,128)(2,1)}, bf16[112,2560]{1,0:T(8,128)(2,1)S(1)}, u32[]{:S(2)}, u32[]{:S(2)}) %collective-permute-start.10) | collective-permute-done | bytes 573472 | tf_op jit(solution)/shard_map/ppermute | solution.py:362
  251.9 3.1 collective-permute-done.11.refs_2_
  255.0 13.9 %collective-permute-done.12.refs_3_ = bf16[112,2560]{1,0:T(8,128)(2,1)S(1)} collective-permute-done((bf16[112,2560]{1,0:T(8,128)(2,1)}, bf16[112,2560]{1,0:T(8,128)(2,1)S(1)}, u32[]{:S(2)}, u32[]{:S(2)}) %collective-permute-start.12) | collective-permute-done | bytes 573472 | tf_op jit(solution)/shard_map/ppermute | solution.py:362
  268.8 0.8 copy-done.12
  269.7 5.9 %combine.5 = bf16[128,2560]{1,0:T(8,128)(2,1)} custom-call(s32[2]{0:T(128)} %pad_add_fusion.me_ref, bf16[112,2560]{1,0:T(8,128)(2,1)} %get-tuple-element.51.refs_0_, bf16[112,2560]{1,0:T(8,128)(2,1)} %copy-done.10, bf16[112,2560]{1,0:T(8,128)(2,1)} %copy-done.11, bf16[112,2560]{1,0:T(8,128)(2,1)} %copy-done.12, ...), custom_call_target="tpu_custom_call" | custom-call | tf_op jit(solution)/shard_map/combine/pallas_call | solution.py:194
  275.5 1.1 fusion
  276.8 3.0 collective-permute-start.18
  279.7 7.0 %collective-permute-done.17.refs_6_ = bf16[64,2560]{1,0:T(8,128)(2,1)S(1)} collective-permute-done((bf16[64,2560]{1,0:T(8,128)(2,1)S(1)}, bf16[64,2560]{1,0:T(8,128)(2,1)S(1)}, u32[]{:S(2)}, u32[]{:S(2)}) %collective-permute-start.17) | collective-permute-done | bytes 327712 | tf_op jit(solution)/shard_map/ppermute | solution.py:362
  286.8 0.7 copy-done.28
  287.5 0.7 copy-done.29
  288.2 6.5 %combine.6 = (bf16[128,2560]{1,0:T(8,128)(2,1)}, bf16[128,2560]{1,0:T(8,128)(2,1)}) custom-call(s32[2]{0:T(128)} %pad_add_fusion.me_ref, bf16[112,2560]{1,0:T(8,128)(2,1)} %get-tuple-element.51.refs_0_, bf16[112,2560]{1,0:T(8,128)(2,1)} %copy-done.10, bf16[112,2560]{1,0:T(8,128)(2,1)} %copy-done.11, bf16[112,2560]{1,0:T(8,128)(2,1)} %copy-done.12, ...), custom_call_target="tpu_custom_call" | custom-call | tf_op jit(solution)/shard_map/combine/pallas_call | solution.py:194
  294.7 0.7 collective-permute-start.19
  295.5 2.0 collective-permute-start.20
  297.5 0.8 collective-permute-start.6
  298.3 0.9 collective-permute-start.7
  299.2 7.6 %collective-permute-done.5.refs_1_ = bf16[80,2560]{1,0:T(8,128)(2,1)S(1)} collective-permute-done((bf16[80,2560]{1,0:T(8,128)(2,1)}, bf16[80,2560]{1,0:T(8,128)(2,1)S(1)}, u32[]{:S(2)}, u32[]{:S(2)}) %collective-permute-start.5) | collective-permute-done | bytes 409632 | tf_op jit(solution)/shard_map/ppermute | solution.py:362
  306.8 1.3 collective-permute-done.6.refs_2_
  308.1 11.0 %collective-permute-done.7.refs_3_ = bf16[80,2560]{1,0:T(8,128)(2,1)S(1)} collective-permute-done((bf16[80,2560]{1,0:T(8,128)(2,1)S(1)}, bf16[80,2560]{1,0:T(8,128)(2,1)S(1)}, u32[]{:S(2)}, u32[]{:S(2)}) %collective-permute-start.7) | collective-permute-done | bytes 409632 | tf_op jit(solution)/shard_map/ppermute | solution.py:362
  320.3 6.6 %combine.7 = (bf16[128,2560]{1,0:T(8,128)(2,1)}, bf16[128,2560]{1,0:T(8,128)(2,1)}) custom-call(s32[2]{0:T(128)} %pad_add_fusion.me_ref, bf16[80,2560]{1,0:T(8,128)(2,1)} %get-tuple-element.47.refs_0_, bf16[80,2560]{1,0:T(8,128)(2,1)} %copy-done.22, bf16[80,2560]{1,0:T(8,128)(2,1)} %copy-done.23, bf16[80,2560]{1,0:T(8,128)(2,1)} %copy-done.24, ...), custom_call_target="tpu_custom_call" | custom-call | tf_op jit(solution)/shard_map/combine/pallas_call | solution.py:194
  327.0 2.7 collective-permute-start.22
  329.6 0.8 collective-permute-start.1
  330.5 0.9 collective-permute-start.2
  331.3 12.0 %collective-permute-done.refs_1_ = bf16[112,2560]{1,0:T(8,128)(2,1)S(1)} collective-permute-done((bf16[112,2560]{1,0:T(8,128)(2,1)}, bf16[112,2560]{1,0:T(8,128)(2,1)S(1)}, u32[]{:S(2)}, u32[]{:S(2)}) %collective-permute-start) | collective-permute-done | bytes 573472 | tf_op jit(solution)/shard_map/ppermute | solution.py:362
  343.4 15.1 %collective-permute-done.2.refs_3_ = bf16[112,2560]{1,0:T(8,128)(2,1)S(1)} collective-permute-done((bf16[112,2560]{1,0:T(8,128)(2,1)}, bf16[112,2560]{1,0:T(8,128)(2,1)S(1)}, u32[]{:S(2)}, u32[]{:S(2)}) %collective-permute-start.2) | collective-permute-done | bytes 573472 | tf_op jit(solution)/shard_map/ppermute | solution.py:362
  358.6 0.8 copy-done.9
  359.8 6.8 %combine.8 = (bf16[128,2560]{1,0:T(8,128)(2,1)}, bf16[128,2560]{1,0:T(8,128)(2,1)}) custom-call(s32[2]{0:T(128)} %pad_add_fusion.me_ref, bf16[112,2560]{1,0:T(8,128)(2,1)} %get-tuple-element.43.refs_0_, bf16[112,2560]{1,0:T(8,128)(2,1)} %copy-done.7, bf16[112,2560]{1,0:T(8,128)(2,1)} %copy-done.8, bf16[112,2560]{1,0:T(8,128)(2,1)} %copy-done.9, ...), custom_call_target="tpu_custom_call" | custom-call | tf_op jit(solution)/shard_map/combine/pallas_call | solution.py:194
  366.6 2.7 collective-permute-start.24
  369.3 14.5 %collective-permute-done.23.refs_5_ = bf16[128,2560]{1,0:T(8,128)(2,1)S(1)} collective-permute-done((bf16[128,2560]{1,0:T(8,128)(2,1)}, bf16[128,2560]{1,0:T(8,128)(2,1)S(1)}, u32[]{:S(2)}, u32[]{:S(2)}) %collective-permute-start.23) | collective-permute-done | bytes 655392 | tf_op jit(solution)/shard_map/ppermute | solution.py:362
  383.8 0.8 copy-done.17
  384.7 0.9 copy-done.18
  385.5 6.1 %combine.9 = bf16[128,2560]{1,0:T(8,128)(2,1)} custom-call(s32[2]{0:T(128)} %pad_add_fusion.me_ref, bf16[112,2560]{1,0:T(8,128)(2,1)} %get-tuple-element.43.refs_0_, bf16[112,2560]{1,0:T(8,128)(2,1)} %copy-done.7, bf16[112,2560]{1,0:T(8,128)(2,1)} %copy-done.8, bf16[112,2560]{1,0:T(8,128)(2,1)} %copy-done.9, bf16[128,2688]{1,0:T(8,128)(2,1)} %prep.1.refs_4_.refs_0_.refs_3_, ...), custom_call_target="tpu_custom_call" | custom-call | tf_op jit(solution)/shard_map/combine/pallas_call | solution.py:194
  391.7 4.3 %copy.15 = bf16[1,2560,768]{2,1,0:T(8,128)(2,1)} copy(bf16[1,2560,768]{2,1,0:T(8,128)(2,1)} %bitcast.14) | data formatting | bytes 7864320
  (95 shorter events, 5.2 us)
Async XLA Ops:
  7.2 213.3 %all-gather.6.cloned.1.call-start = ((), (), s32[]{:S(2)}) async-start(), calls=%async_computation.2 | async-start | bytes 4423680 | tf_op jit(solution)/shard_map/all_gather | solution.py:366
  11.3 21.7 %collective-permute-start.4 = (bf16[128,2688]{1,0:T(8,128)(2,1)}, bf16[128,2688]{1,0:T(8,128)(2,1)S(1)}, u32[]{:S(2)}, u32[]{:S(2)}) collective-permute-start(bf16[128,2688]{1,0:T(8,128)(2,1)} %prep.1.refs_4_.refs_0_.refs_3_), channel_id=1, source_target_pairs={{0,8},{8,16},{16,24},{24,32},{32,40},{40,48},{48,56},{56,0},{1,9},... | collective-permute-start | bytes 2064392 | tf_op jit(solution)/shard_map/ppermute | solution.py:362
  13.8 19.3 %collective-permute-start.3 = (bf16[128,2688]{1,0:T(8,128)(2,1)}, bf16[128,2688]{1,0:T(8,128)(2,1)S(1)}, u32[]{:S(2)}, u32[]{:S(2)}) collective-permute-start(bf16[128,2688]{1,0:T(8,128)(2,1)} %prep.1.refs_4_.refs_0_.refs_3_), channel_id=1, source_target_pairs={{0,56},{8,0},{16,8},{24,16},{32,24},{40,32},{48,40},{56,48},{1,57}... | collective-permute-start | bytes 2064392 | tf_op jit(solution)/shard_map/ppermute | solution.py:362
  33.1 34.5 %copy-start.4 = (bf16[128,2688]{1,0:T(8,128)(2,1)}, bf16[128,2688]{1,0:T(8,128)(2,1)S(1)}, u32[]{:S(2)}) copy-start(bf16[128,2688]{1,0:T(8,128)(2,1)S(1)} %collective-permute-done.4.refs_5_.refs_1_.refs_4_) | copy-start | bytes 2064388
  33.1 17.0 %collective-permute-start.9 = (bf16[128,2688]{1,0:T(8,128)(2,1)S(1)}, bf16[128,2688]{1,0:T(8,128)(2,1)S(1)}, u32[]{:S(2)}, u32[]{:S(2)}) collective-permute-start(bf16[128,2688]{1,0:T(8,128)(2,1)S(1)} %collective-permute-done.4.refs_5_.refs_1_.refs_4_), channel_id=1, source_target_pairs={{0,8},{8,16},{16,24},{24,32},{32,40},{40,48},{48,56},{56,0},{1,9},... | collective-permute-start | bytes 2064392 | tf_op jit(solution)/shard_map/ppermute | solution.py:362
  33.1 17.0 %copy-start.5 = (bf16[128,2688]{1,0:T(8,128)(2,1)}, bf16[128,2688]{1,0:T(8,128)(2,1)S(1)}, u32[]{:S(2)}) copy-start(bf16[128,2688]{1,0:T(8,128)(2,1)S(1)} %collective-permute-done.3.refs_4_.refs_2_.refs_5_) | copy-start | bytes 2064388
  33.1 16.9 %collective-permute-start.8 = (bf16[128,2688]{1,0:T(8,128)(2,1)S(1)}, bf16[128,2688]{1,0:T(8,128)(2,1)S(1)}, u32[]{:S(2)}, u32[]{:S(2)}) collective-permute-start(bf16[128,2688]{1,0:T(8,128)(2,1)S(1)} %collective-permute-done.3.refs_4_.refs_2_.refs_5_), channel_id=1, source_target_pairs={{0,56},{8,0},{16,8},{24,16},{32,24},{40,32},{48,40},{56,48},{1,57}... | collective-permute-start | bytes 2064392 | tf_op jit(solution)/shard_map/ppermute | solution.py:362
  50.0 31.4 %copy-start.2 = (bf16[128,2688]{1,0:T(8,128)(2,1)}, bf16[128,2688]{1,0:T(8,128)(2,1)S(1)}, u32[]{:S(2)}) copy-start(bf16[128,2688]{1,0:T(8,128)(2,1)S(1)} %collective-permute-done.9.refs_5_.refs_0_.refs_2_) | copy-start | bytes 2064388
  50.0 16.1 %collective-permute-start.14 = (bf16[128,2688]{1,0:T(8,128)(2,1)S(1)}, bf16[128,2688]{1,0:T(8,128)(2,1)S(1)}, u32[]{:S(2)}, u32[]{:S(2)}) collective-permute-start(bf16[128,2688]{1,0:T(8,128)(2,1)S(1)} %collective-permute-done.9.refs_5_.refs_0_.refs_2_), channel_id=1, source_target_pairs={{0,8},{8,16},{16,24},{24,32},{32,40},{40,48},{48,56},{56,0},{1,9},... | collective-permute-start | bytes 2064392 | tf_op jit(solution)/shard_map/ppermute | solution.py:362
  50.0 31.4 %copy-start.3 = (bf16[128,2688]{1,0:T(8,128)(2,1)}, bf16[128,2688]{1,0:T(8,128)(2,1)S(1)}, u32[]{:S(2)}) copy-start(bf16[128,2688]{1,0:T(8,128)(2,1)S(1)} %collective-permute-done.8.refs_4_.refs_1_.refs_3_) | copy-start | bytes 2064388
  50.0 28.6 %collective-permute-start.13 = (bf16[128,2688]{1,0:T(8,128)(2,1)S(1)}, bf16[128,2688]{1,0:T(8,128)(2,1)S(1)}, u32[]{:S(2)}, u32[]{:S(2)}) collective-permute-start(bf16[128,2688]{1,0:T(8,128)(2,1)S(1)} %collective-permute-done.8.refs_4_.refs_1_.refs_3_), channel_id=1, source_target_pairs={{0,56},{8,0},{16,8},{24,16},{32,24},{40,32},{48,40},{56,48},{1,57}... | collective-permute-start | bytes 2064392 | tf_op jit(solution)/shard_map/ppermute | solution.py:362
  66.1 20.9 %copy-start = (bf16[128,2688]{1,0:T(8,128)(2,1)}, bf16[128,2688]{1,0:T(8,128)(2,1)S(1)}, u32[]{:S(2)}) copy-start(bf16[128,2688]{1,0:T(8,128)(2,1)S(1)} %collective-permute-done.14.refs_5_.refs_0_.refs_4_) | copy-start | bytes 2064388
  66.9 20.1 %collective-permute-start.15 = (bf16[64,2688]{1,0:T(8,128)(2,1)}, bf16[64,2688]{1,0:T(8,128)(2,1)}, u32[]{:S(2)}, u32[]{:S(2)}) collective-permute-start(bf16[64,2688]{1,0:T(8,128)(2,1)} %slice.16), channel_id=1, source_target_pairs={{0,8},{8,16},{16,24},{24,32},{32,40},{40,48},{48,56},{56,0},{1,9},... | collective-permute-start | bytes 1032200 | tf_op jit(solution)/shard_map/ppermute | solution.py:362
  73.8 20.9 %collective-permute-start.25 = (bf16[112,2560]{1,0:T(8,128)(2,1)}, bf16[112,2560]{1,0:T(8,128)(2,1)}, u32[]{:S(2)}, u32[]{:S(2)}) collective-permute-start(bf16[112,2560]{1,0:T(8,128)(2,1)} %get-tuple-element.62), channel_id=1, source_target_pairs={{0,64},{64,128},{128,192},{192,0},{1,65},{65,129},{129,193},{193,1... | collective-permute-start | bytes 1720328 | tf_op jit(solution)/shard_map/ppermute | solution.py:362
  75.1 25.2 %collective-permute-start.26 = (bf16[112,2560]{1,0:T(8,128)(2,1)}, bf16[112,2560]{1,0:T(8,128)(2,1)}, u32[]{:S(2)}, u32[]{:S(2)}) collective-permute-start(bf16[112,2560]{1,0:T(8,128)(2,1)} %get-tuple-element.63), channel_id=1, source_target_pairs={{0,128},{64,192},{128,0},{192,64},{1,129},{65,193},{129,1},{193,65... | collective-permute-start | bytes 1720328 | tf_op jit(solution)/shard_map/ppermute | solution.py:362
  77.5 27.6 %collective-permute-start.27 = (bf16[112,2560]{1,0:T(8,128)(2,1)}, bf16[112,2560]{1,0:T(8,128)(2,1)}, u32[]{:S(2)}, u32[]{:S(2)}) collective-permute-start(bf16[112,2560]{1,0:T(8,128)(2,1)} %get-tuple-element.64), channel_id=1, source_target_pairs={{0,192},{64,0},{128,64},{192,128},{1,193},{65,1},{129,65},{193,129... | collective-permute-start | bytes 1720328 | tf_op jit(solution)/shard_map/ppermute | solution.py:362
  78.7 8.8 %copy-start.1 = (bf16[128,2688]{1,0:T(8,128)(2,1)}, bf16[128,2688]{1,0:T(8,128)(2,1)S(1)}, u32[]{:S(2)}) copy-start(bf16[128,2688]{1,0:T(8,128)(2,1)S(1)} %collective-permute-done.13.refs_4_.refs_1_.refs_5_) | copy-start | bytes 2064388
  78.7 8.7 %collective-permute-start.16 = (bf16[64,2688]{1,0:T(8,128)(2,1)S(1)}, bf16[64,2688]{1,0:T(8,128)(2,1)S(1)}, u32[]{:S(2)}, u32[]{:S(2)}) collective-permute-start(bf16[64,2688]{1,0:T(8,128)(2,1)S(1)} %slice.17), channel_id=1, source_target_pairs={{0,56},{8,0},{16,8},{24,16},{32,24},{40,32},{48,40},{56,48},{1,57}... | collective-permute-start | bytes 1032200 | tf_op jit(solution)/shard_map/ppermute | solution.py:362
  87.0 23.2 %collective-permute-start.28 = (bf16[80,2560]{1,0:T(8,128)(2,1)}, bf16[80,2560]{1,0:T(8,128)(2,1)S(1)}, u32[]{:S(2)}, u32[]{:S(2)}) collective-permute-start(bf16[80,2560]{1,0:T(8,128)(2,1)} %get-tuple-element.66), channel_id=1, source_target_pairs={{0,64},{64,128},{128,192},{192,0},{1,65},{65,129},{129,193},{193,1... | collective-permute-start | bytes 1228808 | tf_op jit(solution)/shard_map/ppermute | solution.py:362
  94.4 49.8 %collective-permute-start.31 = (bf16[112,2560]{1,0:T(8,128)(2,1)}, bf16[112,2560]{1,0:T(8,128)(2,1)S(1)}, u32[]{:S(2)}, u32[]{:S(2)}) collective-permute-start(bf16[112,2560]{1,0:T(8,128)(2,1)} %get-tuple-element.70), channel_id=1, source_target_pairs={{0,64},{64,128},{128,192},{192,0},{1,65},{65,129},{129,193},{193,1... | collective-permute-start | bytes 1720328 | tf_op jit(solution)/shard_map/ppermute | solution.py:362
  94.7 49.5 %collective-permute-start.32 = (bf16[112,2560]{1,0:T(8,128)(2,1)}, bf16[112,2560]{1,0:T(8,128)(2,1)S(1)}, u32[]{:S(2)}, u32[]{:S(2)}) collective-permute-start(bf16[112,2560]{1,0:T(8,128)(2,1)} %get-tuple-element.71), channel_id=1, source_target_pairs={{0,128},{64,192},{128,0},{192,64},{1,129},{65,193},{129,1},{193,65... | collective-permute-start | bytes 1720328 | tf_op jit(solution)/shard_map/ppermute | solution.py:362
  100.3 44.0 %collective-permute-start.33 = (bf16[112,2560]{1,0:T(8,128)(2,1)}, bf16[112,2560]{1,0:T(8,128)(2,1)S(1)}, u32[]{:S(2)}, u32[]{:S(2)}) collective-permute-start(bf16[112,2560]{1,0:T(8,128)(2,1)} %get-tuple-element.72), channel_id=1, source_target_pairs={{0,192},{64,0},{128,64},{192,128},{1,193},{65,1},{129,65},{193,129... | collective-permute-start | bytes 1720328 | tf_op jit(solution)/shard_map/ppermute | solution.py:362
  105.1 37.2 %collective-permute-start.29 = (bf16[80,2560]{1,0:T(8,128)(2,1)}, bf16[80,2560]{1,0:T(8,128)(2,1)S(1)}, u32[]{:S(2)}, u32[]{:S(2)}) collective-permute-start(bf16[80,2560]{1,0:T(8,128)(2,1)} %get-tuple-element.67), channel_id=1, source_target_pairs={{0,128},{64,192},{128,0},{192,64},{1,129},{65,193},{129,1},{193,65... | collective-permute-start | bytes 1228808 | tf_op jit(solution)/shard_map/ppermute | solution.py:362
  110.2 34.0 %copy-start.25 = (bf16[80,2560]{1,0:T(8,128)(2,1)}, bf16[80,2560]{1,0:T(8,128)(2,1)S(1)}, u32[]{:S(2)}) copy-start(bf16[80,2560]{1,0:T(8,128)(2,1)S(1)} %collective-permute-done.28.refs_5_) | copy-start | bytes 1228804
  110.2 34.0 %collective-permute-start.30 = (bf16[80,2560]{1,0:T(8,128)(2,1)}, bf16[80,2560]{1,0:T(8,128)(2,1)S(1)}, u32[]{:S(2)}, u32[]{:S(2)}) collective-permute-start(bf16[80,2560]{1,0:T(8,128)(2,1)} %get-tuple-element.68), channel_id=1, source_target_pairs={{0,192},{64,0},{128,64},{192,128},{1,193},{65,1},{129,65},{193,129... | collective-permute-start | bytes 1228808 | tf_op jit(solution)/shard_map/ppermute | solution.py:362
  142.3 2.0 copy-start.26
  144.2 0.9 copy-start.19
  144.2 1.2 copy-start.20
  144.2 1.4 copy-start.21
  158.2 54.7 %all-to-all-start = ((bf16[8,336,768]{2,1,0:T(8,128)(2,1)}), bf16[8,336,768]{2,1,0:T(8,128)(2,1)}, u32[]{:S(2)}, u32[]{:S(2)}) async-start(bf16[8,336,768]{2,1,0:T(8,128)(2,1)} %levels.1), calls=%async_computation | async-start | bytes 8257536 | tf_op jit(solution)/shard_map/all_to_all | solution.py:383
  164.9 226.8 %all-gather.4.cloned.1.call-start = ((), (), s32[]{:S(2)}) async-start(), calls=%async_computation.1 | async-start | bytes 4423680 | tf_op jit(solution)/shard_map/all_gather | solution.py:387
  238.0 13.8 %collective-permute-start.10 = (bf16[112,2560]{1,0:T(8,128)(2,1)}, bf16[112,2560]{1,0:T(8,128)(2,1)S(1)}, u32[]{:S(2)}, u32[]{:S(2)}) collective-permute-start(bf16[112,2560]{1,0:T(8,128)(2,1)} %get-tuple-element.52), channel_id=1, source_target_pairs={{0,192},{64,0},{128,64},{192,128},{1,193},{65,1},{129,65},{193,129... | collective-permute-start | bytes 1720328 | tf_op jit(solution)/shard_map/ppermute | solution.py:362
  239.9 15.0 %collective-permute-start.11 = (bf16[112,2560]{1,0:T(8,128)(2,1)}, bf16[112,2560]{1,0:T(8,128)(2,1)S(1)}, u32[]{:S(2)}, u32[]{:S(2)}) collective-permute-start(bf16[112,2560]{1,0:T(8,128)(2,1)} %get-tuple-element.53), channel_id=1, source_target_pairs={{0,128},{64,192},{128,0},{192,64},{1,129},{65,193},{129,1},{193,65... | collective-permute-start | bytes 1720328 | tf_op jit(solution)/shard_map/ppermute | solution.py:362
  240.8 28.0 %collective-permute-start.12 = (bf16[112,2560]{1,0:T(8,128)(2,1)}, bf16[112,2560]{1,0:T(8,128)(2,1)S(1)}, u32[]{:S(2)}, u32[]{:S(2)}) collective-permute-start(bf16[112,2560]{1,0:T(8,128)(2,1)} %get-tuple-element.54), channel_id=1, source_target_pairs={{0,64},{64,128},{128,192},{192,0},{1,65},{65,129},{129,193},{193,1... | collective-permute-start | bytes 1720328 | tf_op jit(solution)/shard_map/ppermute | solution.py:362
  251.9 17.0 %copy-start.10 = (bf16[112,2560]{1,0:T(8,128)(2,1)}, bf16[112,2560]{1,0:T(8,128)(2,1)S(1)}, u32[]{:S(2)}) copy-start(bf16[112,2560]{1,0:T(8,128)(2,1)S(1)} %collective-permute-done.10.refs_1_) | copy-start | bytes 1720324
  255.0 13.9 %copy-start.11 = (bf16[112,2560]{1,0:T(8,128)(2,1)}, bf16[112,2560]{1,0:T(8,128)(2,1)S(1)}, u32[]{:S(2)}) copy-start(bf16[112,2560]{1,0:T(8,128)(2,1)S(1)} %collective-permute-done.11.refs_2_) | copy-start | bytes 1720324
  268.8 0.8 copy-start.12
  269.7 27.8 %copy-start.31 = (bf16[80,2560]{1,0:T(8,128)(2,1)S(1)}, bf16[80,2560]{1,0:T(8,128)(2,1)}, u32[]{:S(2)}) copy-start(bf16[80,2560]{1,0:T(8,128)(2,1)} %get-tuple-element.49) | copy-start | bytes 1228804
  269.7 28.6 %copy-start.30 = (bf16[80,2560]{1,0:T(8,128)(2,1)S(1)}, bf16[80,2560]{1,0:T(8,128)(2,1)}, u32[]{:S(2)}) copy-start(bf16[80,2560]{1,0:T(8,128)(2,1)} %get-tuple-element.50) | copy-start | bytes 1228804
  276.7 10.1 %collective-permute-start.17 = (bf16[64,2560]{1,0:T(8,128)(2,1)S(1)}, bf16[64,2560]{1,0:T(8,128)(2,1)S(1)}, u32[]{:S(2)}, u32[]{:S(2)}) collective-permute-start(bf16[64,2560]{1,0:T(8,128)(2,1)S(1)} %get-tuple-element.77), channel_id=1, source_target_pairs={{0,8},{8,16},{16,24},{24,32},{32,40},{40,48},{48,56},{56,0},{1,9},... | collective-permute-start | bytes 983048 | tf_op jit(solution)/shard_map/ppermute | solution.py:362
  276.8 10.0 %collective-permute-start.18 = (bf16[64,2560]{1,0:T(8,128)(2,1)S(1)}, bf16[64,2560]{1,0:T(8,128)(2,1)S(1)}, u32[]{:S(2)}, u32[]{:S(2)}) collective-permute-start(bf16[64,2560]{1,0:T(8,128)(2,1)S(1)} %get-tuple-element.76), channel_id=1, source_target_pairs={{0,56},{8,0},{16,8},{24,16},{32,24},{40,32},{48,40},{56,48},{1,57}... | collective-permute-start | bytes 983048 | tf_op jit(solution)/shard_map/ppermute | solution.py:362
  294.7 24.4 %collective-permute-start.19 = (bf16[128,2560]{1,0:T(8,128)(2,1)}, bf16[128,2560]{1,0:T(8,128)(2,1)S(1)}, u32[]{:S(2)}, u32[]{:S(2)}) collective-permute-start(bf16[128,2560]{1,0:T(8,128)(2,1)} %get-tuple-element.55), channel_id=1, source_target_pairs={{0,8},{8,16},{16,24},{24,32},{32,40},{40,48},{48,56},{56,0},{1,9},... | collective-permute-start | bytes 1966088 | tf_op jit(solution)/shard_map/ppermute | solution.py:362
  295.5 23.7 %collective-permute-start.20 = (bf16[128,2560]{1,0:T(8,128)(2,1)}, bf16[128,2560]{1,0:T(8,128)(2,1)S(1)}, u32[]{:S(2)}, u32[]{:S(2)}) collective-permute-start(bf16[128,2560]{1,0:T(8,128)(2,1)} %get-tuple-element.56), channel_id=1, source_target_pairs={{0,56},{8,0},{16,8},{24,16},{32,24},{40,32},{48,40},{56,48},{1,57}... | collective-permute-start | bytes 1966088 | tf_op jit(solution)/shard_map/ppermute | solution.py:362
  297.5 9.3 %collective-permute-start.5 = (bf16[80,2560]{1,0:T(8,128)(2,1)}, bf16[80,2560]{1,0:T(8,128)(2,1)S(1)}, u32[]{:S(2)}, u32[]{:S(2)}) collective-permute-start(bf16[80,2560]{1,0:T(8,128)(2,1)} %get-tuple-element.48), channel_id=1, source_target_pairs={{0,192},{64,0},{128,64},{192,128},{1,193},{65,1},{129,65},{193,129... | collective-permute-start | bytes 1228808 | tf_op jit(solution)/shard_map/ppermute | solution.py:362
  297.5 10.7 %collective-permute-start.6 = (bf16[80,2560]{1,0:T(8,128)(2,1)S(1)}, bf16[80,2560]{1,0:T(8,128)(2,1)S(1)}, u32[]{:S(2)}, u32[]{:S(2)}) collective-permute-start(bf16[80,2560]{1,0:T(8,128)(2,1)S(1)} %copy-done.31), channel_id=1, source_target_pairs={{0,128},{64,192},{128,0},{192,64},{1,129},{65,193},{129,1},{193,65... | collective-permute-start | bytes 1228808 | tf_op jit(solution)/shard_map/ppermute | solution.py:362
  298.3 20.8 %collective-permute-start.7 = (bf16[80,2560]{1,0:T(8,128)(2,1)S(1)}, bf16[80,2560]{1,0:T(8,128)(2,1)S(1)}, u32[]{:S(2)}, u32[]{:S(2)}) collective-permute-start(bf16[80,2560]{1,0:T(8,128)(2,1)S(1)} %copy-done.30), channel_id=1, source_target_pairs={{0,64},{64,128},{128,192},{192,0},{1,65},{65,129},{129,193},{193,1... | collective-permute-start | bytes 1228808 | tf_op jit(solution)/shard_map/ppermute | solution.py:362
  306.8 12.4 %copy-start.22 = (bf16[80,2560]{1,0:T(8,128)(2,1)}, bf16[80,2560]{1,0:T(8,128)(2,1)S(1)}, u32[]{:S(2)}) copy-start(bf16[80,2560]{1,0:T(8,128)(2,1)S(1)} %collective-permute-done.5.refs_1_) | copy-start | bytes 1228804
  308.1 11.0 %copy-start.23 = (bf16[80,2560]{1,0:T(8,128)(2,1)}, bf16[80,2560]{1,0:T(8,128)(2,1)S(1)}, u32[]{:S(2)}) copy-start(bf16[80,2560]{1,0:T(8,128)(2,1)S(1)} %collective-permute-done.6.refs_2_) | copy-start | bytes 1228804
  319.1 1.0 copy-start.13
  319.1 1.2 copy-start.15
  326.9 31.6 %collective-permute-start.21 = (bf16[128,2560]{1,0:T(8,128)(2,1)}, bf16[128,2560]{1,0:T(8,128)(2,1)S(1)}, u32[]{:S(2)}, u32[]{:S(2)}) collective-permute-start(bf16[128,2560]{1,0:T(8,128)(2,1)} %get-tuple-element.57), channel_id=1, source_target_pairs={{0,8},{8,16},{16,24},{24,32},{32,40},{40,48},{48,56},{56,0},{1,9},... | collective-permute-start | bytes 1966088 | tf_op jit(solution)/shard_map/ppermute | solution.py:362
  327.0 31.6 %collective-permute-start.22 = (bf16[128,2560]{1,0:T(8,128)(2,1)}, bf16[128,2560]{1,0:T(8,128)(2,1)S(1)}, u32[]{:S(2)}, u32[]{:S(2)}) collective-permute-start(bf16[128,2560]{1,0:T(8,128)(2,1)} %get-tuple-element.58), channel_id=1, source_target_pairs={{0,56},{8,0},{16,8},{24,16},{32,24},{40,32},{48,40},{56,48},{1,57}... | collective-permute-start | bytes 1966088 | tf_op jit(solution)/shard_map/ppermute | solution.py:362
  329.6 13.7 %collective-permute-start = (bf16[112,2560]{1,0:T(8,128)(2,1)}, bf16[112,2560]{1,0:T(8,128)(2,1)S(1)}, u32[]{:S(2)}, u32[]{:S(2)}) collective-permute-start(bf16[112,2560]{1,0:T(8,128)(2,1)} %get-tuple-element.44), channel_id=1, source_target_pairs={{0,192},{64,0},{128,64},{192,128},{1,193},{65,1},{129,65},{193,129... | collective-permute-start | bytes 1720328 | tf_op jit(solution)/shard_map/ppermute | solution.py:362
  329.6 13.8 %collective-permute-start.1 = (bf16[112,2560]{1,0:T(8,128)(2,1)}, bf16[112,2560]{1,0:T(8,128)(2,1)S(1)}, u32[]{:S(2)}, u32[]{:S(2)}) collective-permute-start(bf16[112,2560]{1,0:T(8,128)(2,1)} %get-tuple-element.45), channel_id=1, source_target_pairs={{0,128},{64,192},{128,0},{192,64},{1,129},{65,193},{129,1},{193,65... | collective-permute-start | bytes 1720328 | tf_op jit(solution)/shard_map/ppermute | solution.py:362
  330.5 28.1 %collective-permute-start.2 = (bf16[112,2560]{1,0:T(8,128)(2,1)}, bf16[112,2560]{1,0:T(8,128)(2,1)S(1)}, u32[]{:S(2)}, u32[]{:S(2)}) collective-permute-start(bf16[112,2560]{1,0:T(8,128)(2,1)} %get-tuple-element.46), channel_id=1, source_target_pairs={{0,64},{64,128},{128,192},{192,0},{1,65},{65,129},{129,193},{193,1... | collective-permute-start | bytes 1720328 | tf_op jit(solution)/shard_map/ppermute | solution.py:362
  343.3 15.2 %copy-start.7 = (bf16[112,2560]{1,0:T(8,128)(2,1)}, bf16[112,2560]{1,0:T(8,128)(2,1)S(1)}, u32[]{:S(2)}) copy-start(bf16[112,2560]{1,0:T(8,128)(2,1)S(1)} %collective-permute-done.refs_1_) | copy-start | bytes 1720324
  343.4 15.2 %copy-start.8 = (bf16[112,2560]{1,0:T(8,128)(2,1)}, bf16[112,2560]{1,0:T(8,128)(2,1)S(1)}, u32[]{:S(2)}) copy-start(bf16[112,2560]{1,0:T(8,128)(2,1)S(1)} %collective-permute-done.1.refs_2_) | copy-start | bytes 1720324
  358.5 0.8 copy-start.9
  358.6 1.0 copy-start.14
  358.6 1.2 copy-start.16
  366.6 17.2 %collective-permute-start.23 = (bf16[128,2560]{1,0:T(8,128)(2,1)}, bf16[128,2560]{1,0:T(8,128)(2,1)S(1)}, u32[]{:S(2)}, u32[]{:S(2)}) collective-permute-start(bf16[128,2560]{1,0:T(8,128)(2,1)} %get-tuple-element.59), channel_id=1, source_target_pairs={{0,8},{8,16},{16,24},{24,32},{32,40},{40,48},{48,56},{56,0},{1,9},... | collective-permute-start | bytes 1966088 | tf_op jit(solution)/shard_map/ppermute | solution.py:362
  366.6 17.2 %collective-permute-start.24 = (bf16[128,2560]{1,0:T(8,128)(2,1)}, bf16[128,2560]{1,0:T(8,128)(2,1)S(1)}, u32[]{:S(2)}, u32[]{:S(2)}) collective-permute-start(bf16[128,2560]{1,0:T(8,128)(2,1)} %get-tuple-element.60), channel_id=1, source_target_pairs={{0,56},{8,0},{16,8},{24,16},{32,24},{40,32},{48,40},{56,48},{1,57}... | collective-permute-start | bytes 1966088 | tf_op jit(solution)/shard_map/ppermute | solution.py:362
  383.8 0.8 copy-start.17
  384.7 0.9 copy-start.18
  (5 other events, 3.7 us)
Sparse Core Ops, SparseCore 0:
  13.9 36.3 all-gather.5
  220.6 31.2 all-gather.3

commit v2 on v1

v2 whole, which is shorter than its diff:
```python
import jax
import jax.numpy as jnp
from jax import lax
from jax.experimental import pallas as pl
from jax.experimental.pallas import tpu as pltpu
from jax.sharding import Mesh, PartitionSpec as P

D = 2560
FF = 768
TOP = 6
QB = 128
NQ = FF // QB
STEP = 20
TOK = 128
CAP = 36
NX = 4
NZ = 8
NDP = 8
SHARD = D // NDP
INFO = 128
EXT = D + INFO
MSG = SHARD + 16
TILE = 512

learn_rate = 0.001
beta_one = 0.9
beta_two = 0.999
decay_rate = 0.1
adam_eps = 1e-08
quant_top = 127.0
amax_eps = 1e-06

CHUNKS = ((0, -1, 1), (-2, 2), (-3, 3, 4))
ROWS = tuple(-(-len(c) * CAP // 16) * 16 for c in CHUNKS)
bf16 = jnp.bfloat16
f32 = jnp.float32


VMEM = pltpu.MemorySpace.VMEM
SMEM_SPEC = pl.BlockSpec(memory_space=pltpu.MemorySpace.SMEM)
VMEM_SPEC = pl.BlockSpec(memory_space=VMEM)
STARTS = tuple(NX * sum(ROWS[:c]) for c in range(len(ROWS)))
ALL_ROWS = NX * sum(ROWS)


def params(n=0, mib=6):
    if n == 0:
        return pltpu.CompilerParams(vmem_limit_bytes=mib << 20)
    return pltpu.CompilerParams(
        dimension_semantics=("arbitrary",) * n, vmem_limit_bytes=mib << 20
    )


def near(arrays):
    return [pltpu.with_memory_space_constraint(a, VMEM) for a in arrays]


def prep_kernel(routing_ref, tokens_ref, ext_ref):
    r = routing_ref[...]
    down = lax.broadcasted_iota(jnp.int32, (INFO, TOK), 0)
    across = lax.broadcasted_iota(jnp.int32, (INFO, TOK), 1)
    named = jnp.zeros((INFO, TOK), f32)
    for k in range(TOP):
        named = named + jnp.where(r[k : k + 1, :] == down, 1.0, 0.0)
    earlier = jnp.where(down < across, 1.0, 0.0).astype(bf16)
    before = jnp.dot(named.astype(bf16), earlier, preferred_element_type=f32)
    info = jnp.zeros((INFO, TOK), f32)
    for k in range(TOP):
        e = r[k : k + 1, :]
        w = jnp.sum(jnp.where(e == down, before, 0.0), axis=0, keepdims=True)
        info = jnp.where(down == k, e.astype(f32), info)
        info = jnp.where(down == TOP + k, w, info)
    ext_ref[:, :D] = tokens_ref[...]
    ext_ref[:, D:] = jnp.transpose(info).astype(bf16)


def prep(routing, tokens):
    return pl.pallas_call(
        prep_kernel,
        out_shape=pltpu.VMEM((TOK, EXT), bf16),
        in_specs=[VMEM_SPEC] * 2,
        out_specs=VMEM_SPEC,
        compiler_params=params(),
        name="prep",
    )(routing, tokens)


def joined(parts):
    return parts[0] if len(parts) == 1 else jnp.concatenate(parts, axis=0)


def slot_of(e, w, x, z):
    ex = jnp.floor(e * 0.125)
    ez = e - ex * 8.0
    dx = ex - x
    dx = jnp.where(dx < 0.0, dx + float(NX), dx)
    return jnp.where(ez == z, dx * 64.0 + w, -1.0)


def dispatch(me, blocks, rows):
    nb = len(blocks)
    flat = [a for b in blocks for a in b]
    sizes = [len(b) for b in blocks]
    nf = len(flat)

    def kernel(me_ref, *refs):
        tok, outs, codes, hot = refs[:nf], refs[nf : nf + NX], refs[nf + NX], refs[-1]
        x = me_ref[0].astype(f32)
        z = me_ref[1].astype(f32)
        row = lax.broadcasted_iota(jnp.int32, (rows, TOK), 0).astype(f32)
        at = 0
        for b in range(nb):
            raw = joined([t[:, D:] for t in tok[at : at + sizes[b]]]).astype(f32)
            at += sizes[b]
            codes[b * TOK : (b + 1) * TOK, :] = slot_of(
                raw, pltpu.roll(raw, INFO - TOP, 1), x, z
            ).astype(bf16)
            info = jnp.transpose(raw)
            code = slot_of(info[0:TOP], info[TOP : 2 * TOP], x, z)
            for dx in range(NX):
                want = jnp.where(
                    (row >= float(CAP * b)) & (row < float(CAP * (b + 1))),
                    row - float(CAP * b) + 64.0 * dx,
                    -2.0,
                )
                hit = jnp.zeros((rows, TOK), f32)
                for k in range(TOP):
                    hit = jnp.where(want == code[k : k + 1, :], 1.0, hit)
                hot[dx * rows : (dx + 1) * rows, b * TOK : (b + 1) * TOK] = hit.astype(bf16)

        def column(i, _):
            where = pl.ds(pl.multiple_of(i * TILE, TILE), TILE)
            t = joined([t[:, where] for t in tok])
            got = jnp.dot(hot[...], t, preferred_element_type=f32).astype(bf16)
            for dx in range(NX):
                outs[dx][:, where] = got[dx * rows : (dx + 1) * rows]
            return 0

        lax.fori_loop(0, D // TILE, column, 0)

    out = pl.pallas_call(
        kernel,
        out_shape=[pltpu.VMEM((rows, D), bf16)] * NX
        + [jax.ShapeDtypeStruct((nb * TOK, INFO), bf16)],
        in_specs=[SMEM_SPEC] + [VMEM_SPEC] * nf,
        out_specs=[VMEM_SPEC] * (NX + 1),
        scratch_shapes=[pltpu.VMEM((NX * rows, nb * TOK), bf16)],
        compiler_params=params(),
        name="dispatch",
    )(me, *near(flat))
    return out[:NX], out[NX]


def hots_kernel(*refs):
    nc = len(CHUNKS)
    for c, offsets in enumerate(CHUNKS):
        codes, out, rows = refs[c], refs[nc + c], ROWS[c]
        lane = lax.broadcasted_iota(jnp.int32, (TOK, rows), 1).astype(f32)
        for b in range(len(offsets)):
            code = codes[b * TOK : (b + 1) * TOK, :].astype(f32)
            first = CAP * b
            for dx in range(NX):
                want = jnp.where(
                    (lane >= float(first)) & (lane < float(first + CAP)),
                    lane - float(first) + 64.0 * dx,
                    -2.0,
                )
                hit = jnp.zeros((TOK, rows), f32)
                for k in range(TOP):
                    hit = jnp.where(want == code[:, k : k + 1], 1.0, hit)
                out[b * TOK : (b + 1) * TOK, dx * rows : (dx + 1) * rows] = hit.astype(bf16)


def hots(codes):
    return pl.pallas_call(
        hots_kernel,
        out_shape=[
            pltpu.VMEM((len(o) * TOK, NX * r), bf16) for o, r in zip(CHUNKS, ROWS)
        ],
        in_specs=[VMEM_SPEC] * len(CHUNKS),
        out_specs=[VMEM_SPEC] * len(CHUNKS),
        compiler_params=params(),
        name="hots",
    )(*codes)


def combine(hot, rows_in, slots, adds, last=False, split=1):
    nb = len(slots)
    added = [a for p in adds for a, _ in p]
    na = len(added)

    def kernel(hot_ref, *refs):
        src, extra, outs = refs[:NX], refs[NX : NX + na], refs[NX + na :]

        def column(i, _):
            where = pl.ds(pl.multiple_of(i * TILE, TILE), TILE)
            data = jnp.concatenate([s[:, where] for s in src], axis=0)
            at = 0
            for b in range(nb):
                mine = jnp.dot(
                    hot_ref[slots[b] * TOK : (slots[b] + 1) * TOK, :],
                    data,
                    preferred_element_type=f32,
                )
                for _, (first, count) in adds[b]:
                    more = extra[at][:, where].astype(f32)
                    at += 1
                    if count < TOK:
                        pad = jnp.zeros((TOK - count, TILE), f32)
                        more = jnp.concatenate(
                            [more, pad] if first == 0 else [pad, more], axis=0
                        )
                    mine = mine + more
                mine = mine.astype(bf16)
                part = TOK // split
                for h in range(split):
                    outs[b * split + h][:, where] = mine[h * part : (h + 1) * part]
            return 0

        lax.fori_loop(0, D // TILE, column, 0)

    kind = (lambda s, t: jax.ShapeDtypeStruct(s, t)) if last else pltpu.VMEM
    return pl.pallas_call(
        kernel,
        out_shape=[kind((TOK // split, D), bf16)] * (nb * split),
        in_specs=[VMEM_SPEC] * (1 + NX + na),
        out_specs=[VMEM_SPEC] * (nb * split),
        compiler_params=params(),
        name="combine",
    )(*near([hot, *rows_in, *added]))


def order_kernel(me_ref, up_ref, out):
    x, z = me_ref[0], me_ref[1]
    for c, offsets in enumerate(CHUNKS):
        rows = ROWS[c]
        row = lax.broadcasted_iota(jnp.int32, (rows, NZ * CAP), 0)
        col = lax.broadcasted_iota(jnp.int32, (rows, NZ * CAP), 1)
        want = jnp.full((rows, NZ * CAP), -1, jnp.int32)
        for b, offset in enumerate(offsets):
            block = lax.rem(z + offset + NZ, NZ)
            inside = (row >= CAP * b) & (row < CAP * (b + 1))
            want = jnp.where(inside, block * CAP + row - CAP * b, want)
        pick = jnp.where(want == col, 1.0, 0.0).astype(bf16)
        for dx in range(NX):
            source = lax.rem(x - dx + NX, NX)
            start = pl.multiple_of(source * (NZ * CAP), 16)
            part = up_ref[pl.ds(start, NZ * CAP), :]
            at = STARTS[c] + dx * rows
            out[at : at + rows, :] = jnp.dot(pick, part, preferred_element_type=f32).astype(bf16)


def ordered(me, up):
    return pl.pallas_call(
        order_kernel,
        out_shape=jax.ShapeDtypeStruct((ALL_ROWS, FF), bf16),
        in_specs=[SMEM_SPEC, VMEM_SPEC],
        out_specs=VMEM_SPEC,
        compiler_params=params(),
        name="order",
    )(me, up)


def slot_grads(ups, weights):
    flat_rows = [r for r in ROWS for _ in range(NX)]

    def kernel(up, w, *outs):
        got = lax.dot_general(
            up[...], w[...], (((1,), (1,)), ((), ())), preferred_element_type=f32
        ).astype(bf16)
        at = 0
        for out, r in zip(outs, flat_rows):
            out[...] = got[at : at + r]
            at += r

    out = pl.pallas_call(
        kernel,
        out_shape=[pltpu.HBM((r, D), bf16) for r in flat_rows],
        grid=(D // TILE,),
        in_specs=[
            pl.BlockSpec((ALL_ROWS, FF), lambda i: (0, 0)),
            pl.BlockSpec((TILE, FF), lambda i: (i, 0)),
        ],
        out_specs=[pl.BlockSpec((r, TILE), lambda i: (0, i)) for r in flat_rows],
        compiler_params=params(1, 16),
        name="slot_grads",
    )(ups, weights)
    return [out[c * NX : (c + 1) * NX] for c in range(len(ROWS))]


def levels_of(rows_in, ups, error):
    flat = [a for c in rows_in for a in c]
    wide = 2 * SHARD

    def kernel(*refs):
        src, up, err, out = refs[: len(flat)], refs[-3], refs[-2], refs[-1]
        slab = jnp.concatenate([s[...] for s in src], axis=0)
        total = err[...].astype(f32) + lax.dot_general(
            slab, up[...], (((0,), (0,)), ((), ())), preferred_element_type=f32
        )
        lane = lax.broadcasted_iota(jnp.int32, (wide, QB), 1)
        scales = jnp.zeros((wide, QB), f32)
        for q in range(NQ):
            block = total[:, q * QB : (q + 1) * QB]
            top = jnp.max(jnp.abs(block), axis=1, keepdims=True)
            scale = ((top + amax_eps) / quant_top).astype(bf16).astype(f32)
            level = (block * (1.0 / scale)).astype(bf16)
            out[0, :SHARD, q * QB : (q + 1) * QB] = level[:SHARD]
            out[1, :SHARD, q * QB : (q + 1) * QB] = level[SHARD:]
            scales = jnp.where(lane == q, scale, scales)
        for h in range(2):
            flipped = jnp.transpose(scales[h * SHARD : (h + 1) * SHARD])[:16]
            pad = jnp.zeros((16, FF - SHARD), f32)
            out[h, SHARD:, :] = jnp.concatenate([flipped, pad], axis=1).astype(bf16)

    return pl.pallas_call(
        kernel,
        out_shape=pltpu.HBM((NDP, MSG, FF), bf16),
        grid=(D // wide,),
        in_specs=[pl.BlockSpec((a.shape[0], wide), lambda i: (0, i)) for a in flat]
        + [pl.BlockSpec((ALL_ROWS, FF), lambda i: (0, 0))]
        + [pl.BlockSpec((wide, FF), lambda i: (i, 0))],
        out_specs=pl.BlockSpec((2, MSG, FF), lambda i: (i, 0, 0)),
        compiler_params=params(1, 24),
        name="levels",
    )(*flat, ups, error)


def adam_kernel(loss_ref, got_ref, scale_ref, w_ref, m_ref, v_ref, nw_ref, nm_ref, nv_ref, sc_ref):
    q = pl.program_id(0)

    @pl.when(q == 0)
    def _():
        for d in range(NDP):
            sc_ref[:, d, :] = scale_ref[d].astype(f32)[:, :384]

    scales = jnp.transpose(sc_ref[q])
    total = jnp.zeros((SHARD, QB), f32)
    for d in range(NDP):
        total = total + got_ref[d].astype(f32) * scales[:SHARD, d : d + 1]
    gradient = total / loss_ref[0]
    first = beta_one * m_ref[...].astype(f32) + (1.0 - beta_one) * gradient
    second = beta_two * v_ref[...].astype(f32) + (1.0 - beta_two) * gradient * gradient
    first_hat = first / (1.0 - beta_one**STEP)
    second_hat = second / (1.0 - beta_two**STEP)
    master = w_ref[...].astype(f32)
    updated = master - learn_rate * (
        first_hat / (jnp.sqrt(second_hat) + adam_eps) + decay_rate * master
    )
    nw_ref[0] = updated.astype(bf16)
    nm_ref[...] = first.astype(bf16)
    nv_ref[...] = second.astype(bf16)


def adam(loss, got, w, m, v):
    column = pl.BlockSpec((SHARD, QB), lambda i: (0, i))
    return pl.pallas_call(
        adam_kernel,
        out_shape=[pltpu.HBM((1, SHARD, FF), bf16)]
        + [pltpu.HBM((SHARD, FF), bf16)] * 2,
        grid=(NQ,),
        in_specs=[
            pl.BlockSpec(memory_space=pltpu.SMEM),
            pl.BlockSpec((NDP, SHARD, QB), lambda i: (0, 0, i)),
            pl.BlockSpec((NDP, 16, FF), lambda i: (0, SHARD // 16, 0)),
            column,
            column,
            column,
        ],
        out_specs=[pl.BlockSpec((1, SHARD, QB), lambda i: (0, 0, i)), column, column],
        scratch_shapes=[pltpu.VMEM((16, NDP, 384), f32)],
        compiler_params=params(1, 8),
        name="adam",
    )(loss, got, got, w, m, v)


def step(tokens, routing, grad_up, up_shard, error_feedback, moment_one, moment_two, loss):
    def send(a, axis, n, shift):
        pairs = [(i, (i + shift) % n) for i in range(n)]
        return lax.ppermute(a, axis, pairs)

    def send_x(arrays, sign):
        return [arrays[0]] + [send(arrays[dx], "x", NX, sign * dx) for dx in range(1, NX)]

    def send_z(a, b):
        return send(a, "z", NZ, 1), send(b, "z", NZ, -1)

    me = jnp.stack([lax.axis_index("x"), lax.axis_index("z")]).astype(jnp.int32)
    weights = lax.all_gather(up_shard[0], "dp", axis=0, tiled=True)

    half = TOK // 2
    ext = prep(jnp.transpose(routing), tokens)
    block = {0: [ext]}
    up, down = ext, ext
    for r in (1, 2, 3):
        up, down = send_z(up, down)
        block[-r], block[r] = [up], [down]
    block[4] = list(send_z(up[:half], down[half:]))

    arrived, codes = [], []
    for offsets, rows in zip(CHUNKS, ROWS):
        out, code = dispatch(me, [block[o] for o in offsets], rows)
        arrived.append(send_x(out, 1))
        codes.append(code)
    hot = hots(codes)

    ups = ordered(me, grad_up[0])
    returned = slot_grads(ups, weights)
    packed = levels_of(arrived, ups, error_feedback[0])
    got = lax.all_to_all(packed, "dp", split_axis=0, concat_axis=0, tiled=True)
    new_w, new_m, new_v = adam(loss.reshape(1), got, up_shard[0], moment_one[0], moment_two[0])
    full = lax.all_gather(new_w, "dp", axis=1, tiled=True)

    back = [None] * len(CHUNKS)
    for c in reversed(range(len(CHUNKS))):
        back[c] = send_x(returned[c], -1)
    top, low, whole = (0, half), (half, half), (0, TOK)
    u, d = combine(hot[2], back[2], [2], [[]], split=2)
    u, d = send_z(u, d)
    u, d = combine(hot[2], back[2], [1, 0], [[(u, top)], [(d, low)]])
    u, d = send_z(u, d)
    u, d = combine(hot[1], back[1], [1, 0], [[(u, whole)], [(d, whole)]])
    u, d = send_z(u, d)
    u, d = combine(hot[0], back[0], [2, 1], [[(u, whole)], [(d, whole)]])
    u, d = send_z(u, d)
    (grad_tokens,) = combine(hot[0], back[0], [0], [[(u, whole), (d, whole)]], last=True)
    return (grad_tokens, full, new_m[None], new_v[None])


def solution(mesh):
    fine = Mesh(mesh.devices.reshape(NX, NZ, NDP), ("x", "z", "dp"))
    expert = ("x", "z")
    in_specs = (
        P(("x", "z", "dp"), None),
        P(("x", "z", "dp"), None),
        P(expert, "dp", None),
        P(expert, "dp", None),
        P(expert, "dp", None),
        P(expert, "dp", None),
        P(expert, "dp", None),
        P(),
    )
    out_specs = (
        P(("x", "z", "dp"), None),
        P(expert, None, None),
        P(expert, "dp", None),
        P(expert, "dp", None),
    )
    return jax.shard_map(step, mesh=fine, in_specs=in_specs, out_specs=out_specs, check_vma=False)
```

time: 404 us -> 357 us (0.88)
  Pallas kernels: 94.3 us -> 43.6 us
    pallas_call x13 -> x14, Pallas kernels: 94.3 us -> 43.6 us  [the longest x1 9.5 us: levels_of(): pl.pallas_call(kernel, out_shape=pltpu.HBM((NDP, MSG, FF), bf16), grid=(D...]
    unnamed x66 -> x47, local copies, waits for them, and re-layouts: 14.1 us -> 15.3 us
  transfers between devices with their start and end apart: 37 -> 37, of which waited for: 20 -> 22; matrix products, arithmetic and copies ran while one was open for 1% -> 0% of each run, Pallas kernels for 23% -> 12%
where the time goes in v2:
time: 357 us; the launch traced here: 356 us
  waiting for transfers between devices  232 us (65%)
  starting transfers between devices  50.3 us (14%)
  Pallas kernels  43.6 us (12%)
  local copies, waits for them, and re-layouts  15.4 us (4%)
  between operations  15 us (4%)
    ppermute x34, waiting for transfers between devices, send(): return lax.ppermute(a, axis, pairs)  185 us
    all_to_all x1, waiting for transfers between devices, step(): got = lax.all_to_all(packed, 'dp', split_axis=0, concat_axis=0, tiled=True)  47.4 us
    ppermute x34, starting transfers between devices, send(): return lax.ppermute(a, axis, pairs)  43.5 us
    unnamed x47, local copies, waits for them, and re-layouts  15.3 us
    pallas_call x1, Pallas kernels, levels_of(): pl.pallas_call(kernel, out_shape=pltpu.HBM((NDP, MSG, FF), bf16), grid=(D...  9.5 us
    pallas_call x3, Pallas kernels, dispatch(): pl.pallas_call(kernel, out_shape=[pltpu.VMEM((rows, D), bf16)] * NX + [ja...  8.18 us
    pallas_call x5, Pallas kernels, combine(): pl.pallas_call(kernel, out_shape=[kind((TOK // split, D), bf16)] * (nb *...  7.81 us
    pallas_call x1, Pallas kernels, adam(): pl.pallas_call(adam_kernel, out_shape=[pltpu.HBM((1, SHARD, FF), bf16)] +...  7.34 us
  transfers between devices with their start and end apart: 37, of which 22 were waited for; matrix products, arithmetic and copies ran while one was open for 0% of the time, Pallas kernels for 12%

profile of v2, /device:TPU:1, one launch (start us, length us, event | category | flops | bytes accessed | tf_op | source)
XLA Modules:
  0.0 356.4 jit_solution(10094811830844618333)
XLA Ops:
  7.2 1.1 copy-done.10
  8.3 0.7 copy-done.16
  9.3 6.5 %collective-permute-start.1 = (bf16[128,2688]{1,0:T(8,128)(2,1)S(1)}, bf16[128,2688]{1,0:T(8,128)(2,1)S(1)}, u32[]{:S(2)}, u32[]{:S(2)}) collective-permute-start(bf16[128,2688]{1,0:T(8,128)(2,1)S(1)} %prep.1.refs_0_), channel_id=1, source_target_pairs={{0,56},{8,0},{16,8},{24,16},{32,24},{40,32},{48,40},{56,48},{1,57}... | collective-permute-start | bytes 2064392 | tf_op jit(solution)/shard_map/ppermute | solution.py:380
  15.9 14.0 %collective-permute-done.1.refs_2_ = bf16[128,2688]{1,0:T(8,128)(2,1)S(1)} collective-permute-done((bf16[128,2688]{1,0:T(8,128)(2,1)S(1)}, bf16[128,2688]{1,0:T(8,128)(2,1)S(1)}, u32[]{:S(2)}, u32[]{:S(2)}) %collective-permute-start.1) | collective-permute-done | bytes 688160 | tf_op jit(solution)/shard_map/ppermute | solution.py:380
  29.9 3.4 collective-permute-start.3
  33.3 0.9 copy-done.6
  34.2 0.8 copy-done.8
  35.0 11.5 %collective-permute-done.3.refs_1_ = bf16[128,2688]{1,0:T(8,128)(2,1)S(1)} collective-permute-done((bf16[128,2688]{1,0:T(8,128)(2,1)S(1)}, bf16[128,2688]{1,0:T(8,128)(2,1)S(1)}, u32[]{:S(2)}, u32[]{:S(2)}) %collective-permute-start.3) | collective-permute-done | bytes 688160 | tf_op jit(solution)/shard_map/ppermute | solution.py:380
  46.6 3.4 collective-permute-start.5
  50.6 11.8 %collective-permute-done.5.refs_1_ = bf16[128,2688]{1,0:T(8,128)(2,1)S(1)} collective-permute-done((bf16[128,2688]{1,0:T(8,128)(2,1)S(1)}, bf16[128,2688]{1,0:T(8,128)(2,1)S(1)}, u32[]{:S(2)}, u32[]{:S(2)}) %collective-permute-start.5) | collective-permute-done | bytes 688160 | tf_op jit(solution)/shard_map/ppermute | solution.py:380
  62.4 3.5 collective-permute-start.7
  66.0 1.1 copy-done.7
  67.1 1.1 copy-done.9
  68.2 3.1 dispatch.3
  71.2 1.3 collective-permute-start.25
  72.5 2.4 collective-permute-start.26
  75.0 1.2 collective-permute-start.27
  76.3 2.1 dispatch.4
  79.3 4.6 %collective-permute-done.6.refs_2_ = bf16[64,2688]{1,0:T(8,128)(2,1)S(1)} collective-permute-done((bf16[64,2688]{1,0:T(8,128)(2,1)S(1)}, bf16[64,2688]{1,0:T(8,128)(2,1)S(1)}, u32[]{:S(2)}, u32[]{:S(2)}) %collective-permute-start.6) | collective-permute-done | bytes 344096 | tf_op jit(solution)/shard_map/ppermute | solution.py:380
  83.8 3.1 dispatch.5
  87.1 1.0 collective-permute-start.32
  88.2 8.7 %collective-permute-done.26.refs_2_ = bf16[112,2560]{1,0:T(8,128)(2,1)S(1)} collective-permute-done((bf16[112,2560]{1,0:T(8,128)(2,1)S(1)}, bf16[112,2560]{1,0:T(8,128)(2,1)S(1)}, u32[]{:S(2)}, u32[]{:S(2)}) %collective-permute-start.26) | collective-permute-done | bytes 573472 | tf_op jit(solution)/shard_map/ppermute | solution.py:380
  96.8 6.0 %collective-permute-done.27.refs_3_ = bf16[112,2560]{1,0:T(8,128)(2,1)S(1)} collective-permute-done((bf16[112,2560]{1,0:T(8,128)(2,1)S(1)}, bf16[112,2560]{1,0:T(8,128)(2,1)S(1)}, u32[]{:S(2)}, u32[]{:S(2)}) %collective-permute-start.27) | collective-permute-done | bytes 573472 | tf_op jit(solution)/shard_map/ppermute | solution.py:380
  102.9 1.5 collective-permute-done.28.refs_5_
  104.4 2.4 collective-permute-start.30
  106.8 1.5 copy-done.5
  108.2 1.9 order.1.up.refs_12_
  110.2 28.8 %collective-permute-done.29.refs_6_ = bf16[80,2560]{1,0:T(8,128)(2,1)S(1)} collective-permute-done((bf16[80,2560]{1,0:T(8,128)(2,1)S(1)}, bf16[80,2560]{1,0:T(8,128)(2,1)S(1)}, u32[]{:S(2)}, u32[]{:S(2)}) %collective-permute-start.29) | collective-permute-done | bytes 409632 | tf_op jit(solution)/shard_map/ppermute | solution.py:380
  139.0 2.4 collective-permute-done.30.refs_7_
  141.4 9.5 %levels.1 = bf16[8,336,768]{2,1,0:T(8,128)(2,1)} custom-call(bf16[112,2560]{1,0:T(8,128)(2,1)S(1)} %get-tuple-element.71.refs_0_, bf16[112,2560]{1,0:T(8,128)(2,1)S(1)} %collective-permute-done.25.refs_1_, bf16[112,2560]{1,0:T(8,128)(2,1)S(1)} %collective-permute-done.26.refs_2_, bf16[112,2560]{1,0:T(8,128)(2,1)S(1)} %collective-permute-done.27.refs_3_, ...), custom_call_target="tpu_custom_call" | custom-call | tf_op jit(solution)/shard_map/levels/pallas_call | solution.py:316
  150.9 6.7 %all-to-all-start = ((bf16[8,336,768]{2,1,0:T(8,128)(2,1)}), bf16[8,336,768]{2,1,0:T(8,128)(2,1)}, u32[]{:S(2)}, u32[]{:S(2)}) async-start(bf16[8,336,768]{2,1,0:T(8,128)(2,1)} %levels.1), calls=%async_computation | async-start | bytes 8257536 | tf_op jit(solution)/shard_map/all_to_all | solution.py:410
  158.3 47.4 %all-to-all-done.got_ref.scale_ref = bf16[8,336,768]{2,1,0:T(8,128)(2,1)} async-done(((bf16[8,336,768]{2,1,0:T(8,128)(2,1)}), bf16[8,336,768]{2,1,0:T(8,128)(2,1)}, u32[]{:S(2)}, u32[]{:S(2)}) %all-to-all-start) | async-done | bytes 4128800 | tf_op jit(solution)/shard_map/all_to_all | solution.py:410
  205.7 7.3 %adam.1 = (bf16[1,320,768]{2,1,0:T(8,128)(2,1)}, bf16[320,768]{1,0:T(8,128)(2,1)}, bf16[320,768]{1,0:T(8,128)(2,1)}) custom-call(f32[1]{0:T(128)} %bitcast.12.loss_ref, bf16[8,336,768]{2,1,0:T(8,128)(2,1)} %all-to-all-done.got_ref.scale_ref, bf16[8,336,768]{2,1,0:T(8,128)(2,1)} %all-to-all-done.got_ref.scale_ref, bf16[320,768]{1,0:T(8,128)(2,1)S(1)} %bitcast.15, ...), custom_call_target="tpu_custom_call" | custom-call | tf_op jit(solution)/shard_map/adam/pallas_call | solution.py:357
  213.1 2.1 copy-done
  215.2 6.9 %slot_grads.1 = (bf16[112,2560]{1,0:T(8,128)(2,1)}, bf16[112,2560]{1,0:T(8,128)(2,1)}, bf16[112,2560]{1,0:T(8,128)(2,1)}, bf16[112,2560]{1,0:T(8,128)(2,1)}, bf1...) custom-call(bf16[1216,768]{1,0:T(8,128)(2,1)S(1)} %order.1.up.refs_1, ...), custom_call_target="tpu_custom_call" | custom-call | tf_op jit(solution)/shard_map/slot_grads/pallas_call | solution.py:276
  222.1 2.0 collective-permute-start.14
  224.1 0.9 collective-permute-start.15
  225.4 1.7 hots.1
  227.1 9.0 %collective-permute-done.14.refs_1_ = bf16[112,2560]{1,0:T(8,128)(2,1)S(1)} collective-permute-done((bf16[112,2560]{1,0:T(8,128)(2,1)}, bf16[112,2560]{1,0:T(8,128)(2,1)S(1)}, u32[]{:S(2)}, u32[]{:S(2)}) %collective-permute-start.14) | collective-permute-done | bytes 573472 | tf_op jit(solution)/shard_map/ppermute | solution.py:380
  236.1 3.1 collective-permute-done.15.refs_2_
  239.2 13.9 %collective-permute-done.16.refs_3_ = bf16[112,2560]{1,0:T(8,128)(2,1)S(1)} collective-permute-done((bf16[112,2560]{1,0:T(8,128)(2,1)}, bf16[112,2560]{1,0:T(8,128)(2,1)S(1)}, u32[]{:S(2)}, u32[]{:S(2)}) %collective-permute-start.16) | collective-permute-done | bytes 573472 | tf_op jit(solution)/shard_map/ppermute | solution.py:380
  253.0 1.1 copy-done.3
  254.1 1.2 combine.5
  255.4 2.7 collective-permute-start.18
  258.1 7.3 %collective-permute-done.17.refs_4_ = bf16[64,2560]{1,0:T(8,128)(2,1)S(1)} collective-permute-done((bf16[64,2560]{1,0:T(8,128)(2,1)S(1)}, bf16[64,2560]{1,0:T(8,128)(2,1)S(1)}, u32[]{:S(2)}, u32[]{:S(2)}) %collective-permute-start.17) | collective-permute-done | bytes 327712 | tf_op jit(solution)/shard_map/ppermute | solution.py:380
  265.4 1.6 combine.6
  267.0 2.7 collective-permute-start.20
  269.7 0.9 collective-permute-start.12
  270.6 0.8 collective-permute-start.13
  271.4 7.4 %collective-permute-done.11.refs_1_ = bf16[80,2560]{1,0:T(8,128)(2,1)S(1)} collective-permute-done((bf16[80,2560]{1,0:T(8,128)(2,1)S(1)}, bf16[80,2560]{1,0:T(8,128)(2,1)S(1)}, u32[]{:S(2)}, u32[]{:S(2)}) %collective-permute-start.11) | collective-permute-done | bytes 409632 | tf_op jit(solution)/shard_map/ppermute | solution.py:380
  278.8 1.6 collective-permute-done.12.refs_2_
  280.5 11.0 %collective-permute-done.13.refs_3_ = bf16[80,2560]{1,0:T(8,128)(2,1)S(1)} collective-permute-done((bf16[80,2560]{1,0:T(8,128)(2,1)S(1)}, bf16[80,2560]{1,0:T(8,128)(2,1)S(1)}, u32[]{:S(2)}, u32[]{:S(2)}) %collective-permute-start.13) | collective-permute-done | bytes 409632 | tf_op jit(solution)/shard_map/ppermute | solution.py:380
  291.5 1.5 combine.7
  293.1 2.7 collective-permute-start.22
  295.8 0.9 collective-permute-start.9
  296.7 0.8 collective-permute-start.10
  297.5 11.8 %collective-permute-done.8.refs_1_ = bf16[112,2560]{1,0:T(8,128)(2,1)S(1)} collective-permute-done((bf16[112,2560]{1,0:T(8,128)(2,1)S(1)}, bf16[112,2560]{1,0:T(8,128)(2,1)S(1)}, u32[]{:S(2)}, u32[]{:S(2)}) %collective-permute-start.8) | collective-permute-done | bytes 573472 | tf_op jit(solution)/shard_map/ppermute | solution.py:380
  309.2 0.7 collective-permute-done.9.refs_2_
  309.9 14.6 %collective-permute-done.10.refs_3_ = bf16[112,2560]{1,0:T(8,128)(2,1)S(1)} collective-permute-done((bf16[112,2560]{1,0:T(8,128)(2,1)S(1)}, bf16[112,2560]{1,0:T(8,128)(2,1)S(1)}, u32[]{:S(2)}, u32[]{:S(2)}) %collective-permute-start.10) | collective-permute-done | bytes 573472 | tf_op jit(solution)/shard_map/ppermute | solution.py:380
  324.6 1.6 combine.8
  326.2 2.7 collective-permute-start.24
  328.9 14.3 %collective-permute-done.23.refs_4_ = bf16[128,2560]{1,0:T(8,128)(2,1)S(1)} collective-permute-done((bf16[128,2560]{1,0:T(8,128)(2,1)S(1)}, bf16[128,2560]{1,0:T(8,128)(2,1)S(1)}, u32[]{:S(2)}, u32[]{:S(2)}) %collective-permute-start.23) | collective-permute-done | bytes 655392 | tf_op jit(solution)/shard_map/ppermute | solution.py:380
  343.2 2.0 combine.9
  345.2 4.3 %copy.14 = bf16[1,2560,768]{2,1,0:T(8,128)(2,1)} copy(bf16[1,2560,768]{2,1,0:T(8,128)(2,1)} %all-gather.4.cloned.1.call-done) | data formatting | bytes 7864320
  (76 shorter events, 3.4 us)
Async XLA Ops:
  7.2 205.9 %all-gather.6.cloned.1.call-start = ((), (), s32[]{:S(2)}) async-start(), calls=%async_computation.2 | async-start | bytes 4423680 | tf_op jit(solution)/shard_map/all_gather | solution.py:389
  7.2 1.1 copy-start.10
  8.3 0.7 copy-start.16
  9.3 20.6 %collective-permute-start.1 = (bf16[128,2688]{1,0:T(8,128)(2,1)S(1)}, bf16[128,2688]{1,0:T(8,128)(2,1)S(1)}, u32[]{:S(2)}, u32[]{:S(2)}) collective-permute-start(bf16[128,2688]{1,0:T(8,128)(2,1)S(1)} %prep.1.refs_0_), channel_id=1, source_target_pairs={{0,56},{8,0},{16,8},{24,16},{32,24},{40,32},{48,40},{56,48},{1,57}... | collective-permute-start | bytes 2064392 | tf_op jit(solution)/shard_map/ppermute | solution.py:380
  15.8 18.4 %collective-permute-start = (bf16[128,2688]{1,0:T(8,128)(2,1)S(1)}, bf16[128,2688]{1,0:T(8,128)(2,1)S(1)}, u32[]{:S(2)}, u32[]{:S(2)}) collective-permute-start(bf16[128,2688]{1,0:T(8,128)(2,1)S(1)} %prep.1.refs_0_), channel_id=1, source_target_pairs={{0,8},{8,16},{16,24},{24,32},{32,40},{40,48},{48,56},{56,0},{1,9},... | collective-permute-start | bytes 2064392 | tf_op jit(solution)/shard_map/ppermute | solution.py:380
  29.9 16.7 %collective-permute-start.3 = (bf16[128,2688]{1,0:T(8,128)(2,1)S(1)}, bf16[128,2688]{1,0:T(8,128)(2,1)S(1)}, u32[]{:S(2)}, u32[]{:S(2)}) collective-permute-start(bf16[128,2688]{1,0:T(8,128)(2,1)S(1)} %collective-permute-done.1.refs_2_), channel_id=1, source_target_pairs={{0,56},{8,0},{16,8},{24,16},{32,24},{40,32},{48,40},{56,48},{1,57}... | collective-permute-start | bytes 2064392 | tf_op jit(solution)/shard_map/ppermute | solution.py:380
  33.3 0.9 copy-start.6
  34.2 16.4 %collective-permute-start.2 = (bf16[128,2688]{1,0:T(8,128)(2,1)S(1)}, bf16[128,2688]{1,0:T(8,128)(2,1)S(1)}, u32[]{:S(2)}, u32[]{:S(2)}) collective-permute-start(bf16[128,2688]{1,0:T(8,128)(2,1)S(1)} %collective-permute-done.refs_1_), channel_id=1, source_target_pairs={{0,8},{8,16},{16,24},{24,32},{32,40},{40,48},{48,56},{56,0},{1,9},... | collective-permute-start | bytes 2064392 | tf_op jit(solution)/shard_map/ppermute | solution.py:380
  34.2 0.8 copy-start.8
  46.6 15.8 %collective-permute-start.5 = (bf16[128,2688]{1,0:T(8,128)(2,1)S(1)}, bf16[128,2688]{1,0:T(8,128)(2,1)S(1)}, u32[]{:S(2)}, u32[]{:S(2)}) collective-permute-start(bf16[128,2688]{1,0:T(8,128)(2,1)S(1)} %collective-permute-done.3.refs_1_), channel_id=1, source_target_pairs={{0,56},{8,0},{16,8},{24,16},{32,24},{40,32},{48,40},{56,48},{1,57}... | collective-permute-start | bytes 2064392 | tf_op jit(solution)/shard_map/ppermute | solution.py:380
  50.6 25.6 %collective-permute-start.4 = (bf16[128,2688]{1,0:T(8,128)(2,1)S(1)}, bf16[128,2688]{1,0:T(8,128)(2,1)S(1)}, u32[]{:S(2)}, u32[]{:S(2)}) collective-permute-start(bf16[128,2688]{1,0:T(8,128)(2,1)S(1)} %collective-permute-done.2.refs_0_), channel_id=1, source_target_pairs={{0,8},{8,16},{16,24},{24,32},{32,40},{40,48},{48,56},{56,0},{1,9},... | collective-permute-start | bytes 2064392 | tf_op jit(solution)/shard_map/ppermute | solution.py:380
  62.4 16.6 %collective-permute-start.7 = (bf16[64,2688]{1,0:T(8,128)(2,1)S(1)}, bf16[64,2688]{1,0:T(8,128)(2,1)S(1)}, u32[]{:S(2)}, u32[]{:S(2)}) collective-permute-start(bf16[64,2688]{1,0:T(8,128)(2,1)S(1)} %slice.9), channel_id=1, source_target_pairs={{0,56},{8,0},{16,8},{24,16},{32,24},{40,32},{48,40},{56,48},{1,57}... | collective-permute-start | bytes 1032200 | tf_op jit(solution)/shard_map/ppermute | solution.py:380
  66.0 1.1 copy-start.7
  67.1 1.1 copy-start.9
  71.2 70.2 %copy-start.1 = (bf16[1,2560,768]{2,1,0:T(8,128)(2,1)S(1)}, bf16[1,2560,768]{2,1,0:T(8,128)(2,1)}, u32[]{:S(2)}) copy-start(bf16[1,2560,768]{2,1,0:T(8,128)(2,1)} %param.12) | copy-start | bytes 11796484
  71.2 15.9 %collective-permute-start.25 = (bf16[112,2560]{1,0:T(8,128)(2,1)S(1)}, bf16[112,2560]{1,0:T(8,128)(2,1)S(1)}, u32[]{:S(2)}, u32[]{:S(2)}) collective-permute-start(bf16[112,2560]{1,0:T(8,128)(2,1)S(1)} %get-tuple-element.72), channel_id=1, source_target_pairs={{0,64},{64,128},{128,192},{192,0},{1,65},{65,129},{129,193},{193,1... | collective-permute-start | bytes 1720328 | tf_op jit(solution)/shard_map/ppermute | solution.py:380
  72.5 24.3 %collective-permute-start.26 = (bf16[112,2560]{1,0:T(8,128)(2,1)S(1)}, bf16[112,2560]{1,0:T(8,128)(2,1)S(1)}, u32[]{:S(2)}, u32[]{:S(2)}) collective-permute-start(bf16[112,2560]{1,0:T(8,128)(2,1)S(1)} %get-tuple-element.73), channel_id=1, source_target_pairs={{0,128},{64,192},{128,0},{192,64},{1,129},{65,193},{129,1},{193,65... | collective-permute-start | bytes 1720328 | tf_op jit(solution)/shard_map/ppermute | solution.py:380
  75.0 27.9 %collective-permute-start.27 = (bf16[112,2560]{1,0:T(8,128)(2,1)S(1)}, bf16[112,2560]{1,0:T(8,128)(2,1)S(1)}, u32[]{:S(2)}, u32[]{:S(2)}) collective-permute-start(bf16[112,2560]{1,0:T(8,128)(2,1)S(1)} %get-tuple-element.74), channel_id=1, source_target_pairs={{0,192},{64,0},{128,64},{192,128},{1,193},{65,1},{129,65},{193,129... | collective-permute-start | bytes 1720328 | tf_op jit(solution)/shard_map/ppermute | solution.py:380
  76.2 7.7 %collective-permute-start.6 = (bf16[64,2688]{1,0:T(8,128)(2,1)S(1)}, bf16[64,2688]{1,0:T(8,128)(2,1)S(1)}, u32[]{:S(2)}, u32[]{:S(2)}) collective-permute-start(bf16[64,2688]{1,0:T(8,128)(2,1)S(1)} %slice.8), channel_id=1, source_target_pairs={{0,8},{8,16},{16,24},{24,32},{32,40},{40,48},{48,56},{56,0},{1,9},... | collective-permute-start | bytes 1032200 | tf_op jit(solution)/shard_map/ppermute | solution.py:380
  78.3 0.6 copy-start.14
  79.0 25.4 %collective-permute-start.28 = (bf16[80,2560]{1,0:T(8,128)(2,1)S(1)}, bf16[80,2560]{1,0:T(8,128)(2,1)S(1)}, u32[]{:S(2)}, u32[]{:S(2)}) collective-permute-start(bf16[80,2560]{1,0:T(8,128)(2,1)S(1)} %get-tuple-element.76), channel_id=1, source_target_pairs={{0,64},{64,128},{128,192},{192,0},{1,65},{65,129},{129,193},{193,1... | collective-permute-start | bytes 1228808 | tf_op jit(solution)/shard_map/ppermute | solution.py:380
  86.9 54.5 %collective-permute-start.31 = (bf16[112,2560]{1,0:T(8,128)(2,1)S(1)}, bf16[112,2560]{1,0:T(8,128)(2,1)S(1)}, u32[]{:S(2)}, u32[]{:S(2)}) collective-permute-start(bf16[112,2560]{1,0:T(8,128)(2,1)S(1)} %get-tuple-element.80), channel_id=1, source_target_pairs={{0,64},{64,128},{128,192},{192,0},{1,65},{65,129},{129,193},{193,1... | collective-permute-start | bytes 1720328 | tf_op jit(solution)/shard_map/ppermute | solution.py:380
  87.1 54.2 %collective-permute-start.32 = (bf16[112,2560]{1,0:T(8,128)(2,1)S(1)}, bf16[112,2560]{1,0:T(8,128)(2,1)S(1)}, u32[]{:S(2)}, u32[]{:S(2)}) collective-permute-start(bf16[112,2560]{1,0:T(8,128)(2,1)S(1)} %get-tuple-element.81), channel_id=1, source_target_pairs={{0,128},{64,192},{128,0},{192,64},{1,129},{65,193},{129,1},{193,65... | collective-permute-start | bytes 1720328 | tf_op jit(solution)/shard_map/ppermute | solution.py:380
  96.8 44.5 %collective-permute-start.33 = (bf16[112,2560]{1,0:T(8,128)(2,1)S(1)}, bf16[112,2560]{1,0:T(8,128)(2,1)S(1)}, u32[]{:S(2)}, u32[]{:S(2)}) collective-permute-start(bf16[112,2560]{1,0:T(8,128)(2,1)S(1)} %get-tuple-element.82), channel_id=1, source_target_pairs={{0,192},{64,0},{128,64},{192,128},{1,193},{65,1},{129,65},{193,129... | collective-permute-start | bytes 1720328 | tf_op jit(solution)/shard_map/ppermute | solution.py:380
  102.9 36.1 %collective-permute-start.29 = (bf16[80,2560]{1,0:T(8,128)(2,1)S(1)}, bf16[80,2560]{1,0:T(8,128)(2,1)S(1)}, u32[]{:S(2)}, u32[]{:S(2)}) collective-permute-start(bf16[80,2560]{1,0:T(8,128)(2,1)S(1)} %get-tuple-element.77), channel_id=1, source_target_pairs={{0,128},{64,192},{128,0},{192,64},{1,129},{65,193},{129,1},{193,65... | collective-permute-start | bytes 1228808 | tf_op jit(solution)/shard_map/ppermute | solution.py:380
  104.4 37.0 %collective-permute-start.30 = (bf16[80,2560]{1,0:T(8,128)(2,1)S(1)}, bf16[80,2560]{1,0:T(8,128)(2,1)S(1)}, u32[]{:S(2)}, u32[]{:S(2)}) collective-permute-start(bf16[80,2560]{1,0:T(8,128)(2,1)S(1)} %get-tuple-element.78), channel_id=1, source_target_pairs={{0,192},{64,0},{128,64},{192,128},{1,193},{65,1},{129,65},{193,129... | collective-permute-start | bytes 1228808 | tf_op jit(solution)/shard_map/ppermute | solution.py:380
  106.8 1.5 copy-start.5
  150.9 54.8 %copy-start.4 = (bf16[1,320,768]{2,1,0:T(8,128)(2,1)S(1)}, bf16[1,320,768]{2,1,0:T(8,128)(2,1)}, u32[]{:S(2)}) copy-start(bf16[1,320,768]{2,1,0:T(8,128)(2,1)} %param.11) | copy-start | bytes 1474564
  150.9 54.8 %copy-start.11 = (bf16[1,320,768]{2,1,0:T(8,128)(2,1)S(1)}, bf16[1,320,768]{2,1,0:T(8,128)(2,1)}, u32[]{:S(2)}) copy-start(bf16[1,320,768]{2,1,0:T(8,128)(2,1)} %param.13) | copy-start | bytes 1474564
  150.9 54.8 %copy-start.12 = (bf16[1,320,768]{2,1,0:T(8,128)(2,1)S(1)}, bf16[1,320,768]{2,1,0:T(8,128)(2,1)}, u32[]{:S(2)}) copy-start(bf16[1,320,768]{2,1,0:T(8,128)(2,1)} %param.14) | copy-start | bytes 1474564
  150.9 54.8 %all-to-all-start = ((bf16[8,336,768]{2,1,0:T(8,128)(2,1)}), bf16[8,336,768]{2,1,0:T(8,128)(2,1)}, u32[]{:S(2)}, u32[]{:S(2)}) async-start(bf16[8,336,768]{2,1,0:T(8,128)(2,1)} %levels.1), calls=%async_computation | async-start | bytes 8257536 | tf_op jit(solution)/shard_map/all_to_all | solution.py:410
  157.6 187.6 %all-gather.4.cloned.1.call-start = ((), (), s32[]{:S(2)}) async-start(), calls=%async_computation.1 | async-start | bytes 4423680 | tf_op jit(solution)/shard_map/all_gather | solution.py:412
  213.1 12.3 %copy-start.15 = (bf16[256,128]{1,0:T(8,128)(2,1)S(1)}, bf16[256,128]{1,0:T(8,128)(2,1)}, u32[]{:S(2)}) copy-start(bf16[256,128]{1,0:T(8,128)(2,1)} %copy-done.14) | copy-start | bytes 196612
  213.1 2.1 copy-start
  222.1 13.9 %collective-permute-start.14 = (bf16[112,2560]{1,0:T(8,128)(2,1)}, bf16[112,2560]{1,0:T(8,128)(2,1)S(1)}, u32[]{:S(2)}, u32[]{:S(2)}) collective-permute-start(bf16[112,2560]{1,0:T(8,128)(2,1)} %get-tuple-element.60), channel_id=1, source_target_pairs={{0,192},{64,0},{128,64},{192,128},{1,193},{65,1},{129,65},{193,129... | collective-permute-start | bytes 1720328 | tf_op jit(solution)/shard_map/ppermute | solution.py:380
  224.1 15.0 %collective-permute-start.15 = (bf16[112,2560]{1,0:T(8,128)(2,1)}, bf16[112,2560]{1,0:T(8,128)(2,1)S(1)}, u32[]{:S(2)}, u32[]{:S(2)}) collective-permute-start(bf16[112,2560]{1,0:T(8,128)(2,1)} %get-tuple-element.61), channel_id=1, source_target_pairs={{0,128},{64,192},{128,0},{192,64},{1,129},{65,193},{129,1},{193,65... | collective-permute-start | bytes 1720328 | tf_op jit(solution)/shard_map/ppermute | solution.py:380
  225.0 28.0 %collective-permute-start.16 = (bf16[112,2560]{1,0:T(8,128)(2,1)}, bf16[112,2560]{1,0:T(8,128)(2,1)S(1)}, u32[]{:S(2)}, u32[]{:S(2)}) collective-permute-start(bf16[112,2560]{1,0:T(8,128)(2,1)} %get-tuple-element.62), channel_id=1, source_target_pairs={{0,64},{64,128},{128,192},{192,0},{1,65},{65,129},{129,193},{193,1... | collective-permute-start | bytes 1720328 | tf_op jit(solution)/shard_map/ppermute | solution.py:380
  253.0 1.1 copy-start.3
  254.1 15.6 %copy-start.22 = (bf16[80,2560]{1,0:T(8,128)(2,1)S(1)}, bf16[80,2560]{1,0:T(8,128)(2,1)}, u32[]{:S(2)}) copy-start(bf16[80,2560]{1,0:T(8,128)(2,1)} %get-tuple-element.55) | copy-start | bytes 1228804
  254.1 15.6 %copy-start.21 = (bf16[80,2560]{1,0:T(8,128)(2,1)S(1)}, bf16[80,2560]{1,0:T(8,128)(2,1)}, u32[]{:S(2)}) copy-start(bf16[80,2560]{1,0:T(8,128)(2,1)} %get-tuple-element.56) | copy-start | bytes 1228804
  254.1 16.6 %copy-start.20 = (bf16[80,2560]{1,0:T(8,128)(2,1)S(1)}, bf16[80,2560]{1,0:T(8,128)(2,1)}, u32[]{:S(2)}) copy-start(bf16[80,2560]{1,0:T(8,128)(2,1)} %get-tuple-element.57) | copy-start | bytes 1228804
  254.1 37.4 %copy-start.13 = (bf16[80,2560]{1,0:T(8,128)(2,1)S(1)}, bf16[80,2560]{1,0:T(8,128)(2,1)}, u32[]{:S(2)}) copy-start(bf16[80,2560]{1,0:T(8,128)(2,1)} %get-tuple-element.54.refs_0_) | copy-start | bytes 1228804
  254.1 41.7 %copy-start.19 = (bf16[112,2560]{1,0:T(8,128)(2,1)S(1)}, bf16[112,2560]{1,0:T(8,128)(2,1)}, u32[]{:S(2)}) copy-start(bf16[112,2560]{1,0:T(8,128)(2,1)} %get-tuple-element.50) | copy-start | bytes 1720324
  254.1 41.7 %copy-start.18 = (bf16[112,2560]{1,0:T(8,128)(2,1)S(1)}, bf16[112,2560]{1,0:T(8,128)(2,1)}, u32[]{:S(2)}) copy-start(bf16[112,2560]{1,0:T(8,128)(2,1)} %get-tuple-element.51) | copy-start | bytes 1720324
  254.1 42.6 %copy-start.17 = (bf16[112,2560]{1,0:T(8,128)(2,1)S(1)}, bf16[112,2560]{1,0:T(8,128)(2,1)}, u32[]{:S(2)}) copy-start(bf16[112,2560]{1,0:T(8,128)(2,1)} %get-tuple-element.52) | copy-start | bytes 1720324
  254.1 70.4 %copy-start.2 = (bf16[112,2560]{1,0:T(8,128)(2,1)S(1)}, bf16[112,2560]{1,0:T(8,128)(2,1)}, u32[]{:S(2)}) copy-start(bf16[112,2560]{1,0:T(8,128)(2,1)} %get-tuple-element.49.refs_0_) | copy-start | bytes 1720324
  255.3 10.1 %collective-permute-start.17 = (bf16[64,2560]{1,0:T(8,128)(2,1)S(1)}, bf16[64,2560]{1,0:T(8,128)(2,1)S(1)}, u32[]{:S(2)}, u32[]{:S(2)}) collective-permute-start(bf16[64,2560]{1,0:T(8,128)(2,1)S(1)} %get-tuple-element.63), channel_id=1, source_target_pairs={{0,8},{8,16},{16,24},{24,32},{32,40},{40,48},{48,56},{56,0},{1,9},... | collective-permute-start | bytes 983048 | tf_op jit(solution)/shard_map/ppermute | solution.py:380
  255.4 10.0 %collective-permute-start.18 = (bf16[64,2560]{1,0:T(8,128)(2,1)S(1)}, bf16[64,2560]{1,0:T(8,128)(2,1)S(1)}, u32[]{:S(2)}, u32[]{:S(2)}) collective-permute-start(bf16[64,2560]{1,0:T(8,128)(2,1)S(1)} %get-tuple-element.64), channel_id=1, source_target_pairs={{0,56},{8,0},{16,8},{24,16},{32,24},{40,32},{48,40},{56,48},{1,57}... | collective-permute-start | bytes 983048 | tf_op jit(solution)/shard_map/ppermute | solution.py:380
  266.9 24.5 %collective-permute-start.19 = (bf16[128,2560]{1,0:T(8,128)(2,1)S(1)}, bf16[128,2560]{1,0:T(8,128)(2,1)S(1)}, u32[]{:S(2)}, u32[]{:S(2)}) collective-permute-start(bf16[128,2560]{1,0:T(8,128)(2,1)S(1)} %get-tuple-element.65), channel_id=1, source_target_pairs={{0,8},{8,16},{16,24},{24,32},{32,40},{40,48},{48,56},{56,0},{1,9},... | collective-permute-start | bytes 1966088 | tf_op jit(solution)/shard_map/ppermute | solution.py:380
  267.0 24.4 %collective-permute-start.20 = (bf16[128,2560]{1,0:T(8,128)(2,1)S(1)}, bf16[128,2560]{1,0:T(8,128)(2,1)S(1)}, u32[]{:S(2)}, u32[]{:S(2)}) collective-permute-start(bf16[128,2560]{1,0:T(8,128)(2,1)S(1)} %get-tuple-element.66), channel_id=1, source_target_pairs={{0,56},{8,0},{16,8},{24,16},{32,24},{40,32},{48,40},{56,48},{1,57}... | collective-permute-start | bytes 1966088 | tf_op jit(solution)/shard_map/ppermute | solution.py:380
  269.7 9.1 %collective-permute-start.11 = (bf16[80,2560]{1,0:T(8,128)(2,1)S(1)}, bf16[80,2560]{1,0:T(8,128)(2,1)S(1)}, u32[]{:S(2)}, u32[]{:S(2)}) collective-permute-start(bf16[80,2560]{1,0:T(8,128)(2,1)S(1)} %copy-done.22), channel_id=1, source_target_pairs={{0,192},{64,0},{128,64},{192,128},{1,193},{65,1},{129,65},{193,129... | collective-permute-start | bytes 1228808 | tf_op jit(solution)/shard_map/ppermute | solution.py:380
  269.7 10.8 %collective-permute-start.12 = (bf16[80,2560]{1,0:T(8,128)(2,1)S(1)}, bf16[80,2560]{1,0:T(8,128)(2,1)S(1)}, u32[]{:S(2)}, u32[]{:S(2)}) collective-permute-start(bf16[80,2560]{1,0:T(8,128)(2,1)S(1)} %copy-done.21), channel_id=1, source_target_pairs={{0,128},{64,192},{128,0},{192,64},{1,129},{65,193},{129,1},{193,65... | collective-permute-start | bytes 1228808 | tf_op jit(solution)/shard_map/ppermute | solution.py:380
  270.6 20.8 %collective-permute-start.13 = (bf16[80,2560]{1,0:T(8,128)(2,1)S(1)}, bf16[80,2560]{1,0:T(8,128)(2,1)S(1)}, u32[]{:S(2)}, u32[]{:S(2)}) collective-permute-start(bf16[80,2560]{1,0:T(8,128)(2,1)S(1)} %copy-done.20), channel_id=1, source_target_pairs={{0,64},{64,128},{128,192},{192,0},{1,65},{65,129},{129,193},{193,1... | collective-permute-start | bytes 1228808 | tf_op jit(solution)/shard_map/ppermute | solution.py:380
  293.0 31.5 %collective-permute-start.21 = (bf16[128,2560]{1,0:T(8,128)(2,1)S(1)}, bf16[128,2560]{1,0:T(8,128)(2,1)S(1)}, u32[]{:S(2)}, u32[]{:S(2)}) collective-permute-start(bf16[128,2560]{1,0:T(8,128)(2,1)S(1)} %get-tuple-element.67), channel_id=1, source_target_pairs={{0,8},{8,16},{16,24},{24,32},{32,40},{40,48},{48,56},{56,0},{1,9},... | collective-permute-start | bytes 1966088 | tf_op jit(solution)/shard_map/ppermute | solution.py:380
  293.1 31.5 %collective-permute-start.22 = (bf16[128,2560]{1,0:T(8,128)(2,1)S(1)}, bf16[128,2560]{1,0:T(8,128)(2,1)S(1)}, u32[]{:S(2)}, u32[]{:S(2)}) collective-permute-start(bf16[128,2560]{1,0:T(8,128)(2,1)S(1)} %get-tuple-element.68), channel_id=1, source_target_pairs={{0,56},{8,0},{16,8},{24,16},{32,24},{40,32},{48,40},{56,48},{1,57}... | collective-permute-start | bytes 1966088 | tf_op jit(solution)/shard_map/ppermute | solution.py:380
  295.8 13.5 %collective-permute-start.8 = (bf16[112,2560]{1,0:T(8,128)(2,1)S(1)}, bf16[112,2560]{1,0:T(8,128)(2,1)S(1)}, u32[]{:S(2)}, u32[]{:S(2)}) collective-permute-start(bf16[112,2560]{1,0:T(8,128)(2,1)S(1)} %copy-done.19), channel_id=1, source_target_pairs={{0,192},{64,0},{128,64},{192,128},{1,193},{65,1},{129,65},{193,129... | collective-permute-start | bytes 1720328 | tf_op jit(solution)/shard_map/ppermute | solution.py:380
  295.8 14.2 %collective-permute-start.9 = (bf16[112,2560]{1,0:T(8,128)(2,1)S(1)}, bf16[112,2560]{1,0:T(8,128)(2,1)S(1)}, u32[]{:S(2)}, u32[]{:S(2)}) collective-permute-start(bf16[112,2560]{1,0:T(8,128)(2,1)S(1)} %copy-done.18), channel_id=1, source_target_pairs={{0,128},{64,192},{128,0},{192,64},{1,129},{65,193},{129,1},{193,65... | collective-permute-start | bytes 1720328 | tf_op jit(solution)/shard_map/ppermute | solution.py:380
  296.7 27.8 %collective-permute-start.10 = (bf16[112,2560]{1,0:T(8,128)(2,1)S(1)}, bf16[112,2560]{1,0:T(8,128)(2,1)S(1)}, u32[]{:S(2)}, u32[]{:S(2)}) collective-permute-start(bf16[112,2560]{1,0:T(8,128)(2,1)S(1)} %copy-done.17), channel_id=1, source_target_pairs={{0,64},{64,128},{128,192},{192,0},{1,65},{65,129},{129,193},{193,1... | collective-permute-start | bytes 1720328 | tf_op jit(solution)/shard_map/ppermute | solution.py:380
  326.1 17.1 %collective-permute-start.23 = (bf16[128,2560]{1,0:T(8,128)(2,1)S(1)}, bf16[128,2560]{1,0:T(8,128)(2,1)S(1)}, u32[]{:S(2)}, u32[]{:S(2)}) collective-permute-start(bf16[128,2560]{1,0:T(8,128)(2,1)S(1)} %get-tuple-element.69), channel_id=1, source_target_pairs={{0,8},{8,16},{16,24},{24,32},{32,40},{40,48},{48,56},{56,0},{1,9},... | collective-permute-start | bytes 1966088 | tf_op jit(solution)/shard_map/ppermute | solution.py:380
  326.2 17.0 %collective-permute-start.24 = (bf16[128,2560]{1,0:T(8,128)(2,1)S(1)}, bf16[128,2560]{1,0:T(8,128)(2,1)S(1)}, u32[]{:S(2)}, u32[]{:S(2)}) collective-permute-start(bf16[128,2560]{1,0:T(8,128)(2,1)S(1)} %get-tuple-element.70), channel_id=1, source_target_pairs={{0,56},{8,0},{16,8},{24,16},{32,24},{40,32},{48,40},{56,48},{1,57}... | collective-permute-start | bytes 1966088 | tf_op jit(solution)/shard_map/ppermute | solution.py:380
Sparse Core Ops, SparseCore 0:
  15.9 31.8 all-gather.5
  213.2 29.8 all-gather.3
